TPU v7x, 256 devices: a whole 4x4x8 slice. The times are simulated.
256 devices in a mesh: chan: 2 (over core), ens: 16 (over y, z_lo), lat: 8 (over z_hi, x).
Axes of the slice: x: 4, y: 4, z: 8 (z_hi: 2, z_lo: 4; z = z_hi * 4 + z_lo), core: 2. Of those that a mesh axis runs over, the one named last changes fastest.
Arguments:
- model_outputs: bfloat16 [16, 2, 720, 1440], P('ens', 'chan', 'lat'), may hold values from -340 to 340
- verifying_truth: bfloat16 [2, 720, 1440], P('chan', 'lat', 'ens'), may hold values from -250 to 250
Outputs:
- scaled_gradient: float32 [16, 2, 720, 1440], P('ens', 'chan', 'lat')
- ensemble_loss: float32 [], replicated
All inputs are finite; a program needn't handle non-finite values.
Results may differ from a plain program's by a relative error of at most 0.02.
The roundings to bfloat16 on the way count: a program that leaves them out, or rounds other values in their place, can miss the bound.
Values may be sent and summed in bfloat16 or wider, within the bound.
A program may use at most 64 MiB of HBM per device.

v0:
```python
import math

import jax
import jax.numpy as jnp
from jax import lax
from jax.sharding import PartitionSpec as P

PARALLEL_LINES = 720
AZIMUTH_STEPS = 1440
DEGREE_CUTOFF = 384


SOFTENING_EPS = 0.25
SPECTRAL_WEIGHT = 0.1


def dft_table():
    longitude = jnp.arange(AZIMUTH_STEPS, dtype=jnp.int32)[:, None]
    wavenumber = jnp.arange(DEGREE_CUTOFF, dtype=jnp.int32)[None, :]
    phase = (longitude * wavenumber % AZIMUTH_STEPS).astype(jnp.float32) * (
        2.0 * math.pi / AZIMUTH_STEPS
    )
    stacked = jnp.stack([jnp.cos(phase), -jnp.sin(phase)], axis=-1)
    return stacked.reshape(AZIMUTH_STEPS, 2 * DEGREE_CUTOFF).astype(jnp.bfloat16)


def lat_rows(first_row, count):
    rows_index = (first_row + jnp.arange(count, dtype=jnp.int32)).astype(jnp.float32)
    colatitude = math.pi * (rows_index + 0.5) / PARALLEL_LINES
    return (jnp.cos(colatitude), jnp.sin(colatitude))


def seed_log(order_values):
    factors = jnp.arange(1, DEGREE_CUTOFF + 1, dtype=jnp.int32).astype(jnp.float32)[None, :]
    summands = jnp.where(factors <= order_values[:, None], jnp.log1p(-0.5 / factors), 0.0)
    return 0.5 * jnp.log(order_values + 0.5) + 0.5 * jnp.sum(summands, axis=1)


def legendre_table(order_values, cos_lat, sin_lat):
    order_col = order_values[:, None]
    start_log = seed_log(order_values)[:, None] + order_col * jnp.log(sin_lat)[None, :]
    cos_row = cos_lat[None, :]
    state_shape = (order_values.shape[0], cos_lat.shape[0])

    def recur(carry, degree_index):
        latest, before, log_scale = carry
        degree = degree_index.astype(jnp.float32)
        growing = degree > order_col
        denominator = jnp.where(growing, degree * degree - order_col * order_col, 1.0)
        leading = jnp.sqrt(jnp.maximum(4.0 * degree * degree - 1.0, 0.0) / denominator)
        trailing = jnp.sqrt(
            jnp.maximum(
                ((degree - 1.0) ** 2 - order_col * order_col)
                * (2.0 * degree + 1.0)
                / ((2.0 * degree - 3.0) * denominator),
                0.0,
            )
        )
        advanced = leading * cos_row * latest - trailing * before
        next_latest = jnp.where(growing, advanced, latest)
        next_before = jnp.where(growing, latest, before)
        largest = jnp.maximum(jnp.abs(next_latest), jnp.abs(next_before))
        next_latest = next_latest / largest
        next_before = next_before / largest
        next_log = log_scale + jnp.log(largest)
        value = jnp.where(degree >= order_col, next_latest * jnp.exp(next_log), 0.0)
        return ((next_latest, next_before, next_log), value)

    initial = (
        jnp.ones(state_shape, cos_lat.dtype),
        jnp.zeros(state_shape, cos_lat.dtype),
        start_log,
    )
    unused, stacked = lax.scan(
        recur, initial, jnp.arange(DEGREE_CUTOFF, dtype=jnp.int32), unroll=16
    )
    legendre = jnp.transpose(stacked, (1, 2, 0))
    weights = math.pi / PARALLEL_LINES * sin_lat
    return (weights[None, :, None] * legendre).astype(jnp.bfloat16)


def coefficient_parts(expansion_terms, azimuth_wavenumber, prediction_draws):
    degree = jnp.arange(DEGREE_CUTOFF, dtype=jnp.int32).astype(jnp.float32)
    retained = (degree >= azimuth_wavenumber).astype(jnp.float32)
    draw_stack = expansion_terms[:, :, :prediction_draws]
    pivot_term = expansion_terms[:, :, prediction_draws:]
    observed_gap = draw_stack - pivot_term
    observed_length = jnp.sqrt(observed_gap[0] ** 2 + observed_gap[1] ** 2 + SOFTENING_EPS**2)
    couple_gap = draw_stack[:, :, :, None] - draw_stack[:, :, None]
    couple_length = jnp.sqrt(couple_gap[0] ** 2 + couple_gap[1] ** 2 + SOFTENING_EPS**2)
    power_score = jnp.sum(observed_length, axis=1) - (
        jnp.sum(couple_length, axis=(1, 2)) - prediction_draws * SOFTENING_EPS
    ) / (2.0 * (prediction_draws - 1))
    penalty_piece = jnp.sum(retained * power_score)
    step_downhill = observed_gap / observed_length[None] - jnp.sum(
        couple_gap / couple_length[None], axis=3
    ) / (prediction_draws - 1)
    scale_factor = (
        SPECTRAL_WEIGHT * PARALLEL_LINES * AZIMUTH_STEPS / (DEGREE_CUTOFF * (DEGREE_CUTOFF + 1) / 2)
    )
    return (penalty_piece, (scale_factor * retained * step_downhill).astype(jnp.bfloat16))


def local(model_outputs, verifying_truth):
    ens_size = lax.axis_size("ens")
    lat_size = lax.axis_size("lat")
    groups = ens_size * lat_size
    variable_total = model_outputs.shape[1]
    parallel_circle_slice = model_outputs.shape[2]
    lon_block = verifying_truth.shape[2]
    per_device = DEGREE_CUTOFF // groups
    ens_index = lax.axis_index("ens")
    lat_index = lax.axis_index("lat")
    globe_degree_table = dft_table()
    band_cos, band_sin = lat_rows(lat_index * parallel_circle_slice, parallel_circle_slice)
    device_sample_grid = model_outputs[0]
    lon_table = lax.dynamic_slice_in_dim(globe_degree_table, ens_index * lon_block, lon_block, 0)
    partial_value = jnp.einsum(
        "kq,cjk->qcj", lon_table, verifying_truth, preferred_element_type=jnp.float32
    )
    partial_value = partial_value.reshape(
        ens_size, lat_size, per_device, 2, variable_total, parallel_circle_slice
    )
    summed = lax.psum_scatter(partial_value, "ens", scatter_dimension=0, tiled=True).astype(
        jnp.bfloat16
    )
    outgoing_points = device_sample_grid.reshape(
        variable_total, 1, parallel_circle_slice, ens_size, lon_block
    )
    gathered = lax.all_to_all(
        outgoing_points, "ens", split_axis=3, concat_axis=1, tiled=True
    ).reshape(variable_total, ens_size, parallel_circle_slice * lon_block)
    line_factor = jnp.broadcast_to(band_sin[:, None], (parallel_circle_slice, lon_block)).reshape(
        -1
    )
    target = verifying_truth.reshape(variable_total, parallel_circle_slice * lon_block).astype(
        jnp.float32
    )

    def per_channel(packed):
        gridded_quantity = packed[0].astype(jnp.float32)
        true_gap = gridded_quantity - packed[1][None]
        pair_gap = gridded_quantity[:, None] - gridded_quantity[None]
        tally_numbers = (
            (ens_size - 1) * jnp.sign(true_gap) - jnp.sum(jnp.sign(pair_gap), axis=1)
        ).astype(jnp.bfloat16)
        penalty_piece = jnp.sum(line_factor * jnp.abs(true_gap)) - jnp.sum(
            line_factor * jnp.abs(pair_gap)
        ) / (2.0 * (ens_size - 1))
        return (tally_numbers, penalty_piece)

    tally_numbers, grid_losses = lax.map(per_channel, (gathered, target))
    back_counts = tally_numbers.reshape(
        variable_total, ens_size, parallel_circle_slice, 1, lon_block
    )
    counts_own = lax.all_to_all(
        back_counts, "ens", split_axis=1, concat_axis=3, tiled=True
    ).reshape(variable_total, parallel_circle_slice, AZIMUTH_STEPS)
    grid_local = jnp.sum(grid_losses)
    azimuth_spectra = jnp.einsum(
        "kq,cjk->qcj", globe_degree_table, device_sample_grid, preferred_element_type=jnp.float32
    ).astype(jnp.bfloat16)
    outgoing = azimuth_spectra.reshape(
        groups, per_device, 2, variable_total, 1, parallel_circle_slice
    )
    incoming = lax.all_to_all(outgoing, ("ens", "lat"), split_axis=0, concat_axis=4, tiled=True)
    member_modes = incoming.reshape(per_device, 2, variable_total, ens_size, PARALLEL_LINES)
    truth_modes = lax.all_to_all(
        summed.reshape(lat_size, per_device, 2, variable_total, 1, parallel_circle_slice),
        "lat",
        split_axis=0,
        concat_axis=4,
        tiled=True,
    )
    truth_modes = truth_modes.reshape(per_device, 2, variable_total, 1, PARALLEL_LINES)
    all_modes = jnp.concatenate([member_modes, truth_modes], axis=3).reshape(
        per_device, 2 * variable_total * (ens_size + 1), PARALLEL_LINES
    )
    cos_all, sin_all = lat_rows(0, PARALLEL_LINES)
    orders = (
        (ens_index * lat_size + lat_index) * per_device + jnp.arange(per_device, dtype=jnp.int32)
    ).astype(jnp.float32)
    scaled_result = legendre_table(orders, cos_all, sin_all)
    expansion_terms = jnp.einsum(
        "mrj,mjl->mrl", all_modes, scaled_result, preferred_element_type=jnp.float32
    )
    expansion_terms = expansion_terms.reshape(
        per_device, 2, variable_total, ens_size + 1, DEGREE_CUTOFF
    )
    spec_loss, spec_grad = lax.map(
        lambda packed: coefficient_parts(packed[0], packed[1], ens_size), (expansion_terms, orders)
    )
    backward_map = jnp.einsum(
        "mrl,mjl->mrj",
        spec_grad.reshape(per_device, 2 * variable_total * ens_size, DEGREE_CUTOFF),
        scaled_result,
        preferred_element_type=jnp.float32,
    ).astype(jnp.bfloat16)
    sent_back = backward_map.reshape(
        1, per_device, 2, variable_total, groups, parallel_circle_slice
    )
    returned = lax.all_to_all(sent_back, ("ens", "lat"), split_axis=4, concat_axis=0, tiled=True)
    grid_spec = jnp.einsum(
        "qcj,kq->cjk",
        returned.reshape(2 * DEGREE_CUTOFF, variable_total, parallel_circle_slice),
        globe_degree_table,
        preferred_element_type=jnp.float32,
    )
    local_total = grid_local / (PARALLEL_LINES * AZIMUTH_STEPS) + SPECTRAL_WEIGHT / (
        DEGREE_CUTOFF * (DEGREE_CUTOFF + 1) / 2
    ) * jnp.sum(spec_loss)
    ensemble_loss = lax.psum(local_total, ("chan", "ens", "lat"))
    slope_result = (
        band_sin[None, :, None] * counts_own.astype(jnp.float32) / (ens_size - 1) + grid_spec
    )
    return (slope_result[None], ensemble_loss)


def solution(mesh):
    return jax.shard_map(
        local,
        mesh=mesh,
        in_specs=(P("ens", "chan", "lat", None), P("chan", "lat", "ens")),
        out_specs=(P("ens", "chan", "lat", None), P()),
        check_vma=False,
    )
```

profile of v0, /device:TPU:1, one launch (start us, length us, event | category | flops | bytes accessed | tf_op | source)
XLA Modules:
  0.0 576.9 jit_solution(7043533757094644644)
XLA Ops:
  7.2 10.4 %sine_negate_fusion = (bf16[1440,384,1]{1,0,2:T(8,128)(2,1)}, bf16[1440,384,1]{1,0,2:T(8,128)(2,1)}) fusion(), kind=kLoop, calls=%fused_computation.255 | loop fusion | flops 6635520 | bytes 2211840 | tf_op jit(solution)/shard_map/neg | solution.py:23
  17.6 1.8 maximum_convert_fusion
  19.5 4.9 copy.96
  24.4 5.0 convert_element_type.414
  29.7 1.0 copy.101
  30.8 0.8 convolution_convert_fusion
  31.6 0.8 copy.97
  32.5 16.3 %all-to-all-start.2 = ((bf16[128,3,2,1,1,90]{5,2,1,4,3,0:T(2,128)(2,1)}), bf16[128,3,2,1,1,90]{5,2,1,4,3,0:T(2,128)(2,1)S(1)}, u32[]{:S(2)}, u32[]{:S(2)}) async-start(bf16[128,3,2,1,1,90]{5,2,1,4,3,0:T(2,128)(2,1)} %bitcast.19), calls=%async_computation.2 | async-start | bytes 393216 | tf_op jit(solution)/shard_map/all_to_all | solution.py:166
  49.2 348.2 %while.43 = (s32[]{:T(128)}, f32[3,720]{1,0:T(4,128)S(1)}, f32[3,720]{1,0:T(4,128)S(1)}, f32[3,720]{1,0:T(4,128)S(1)}, f32[24,16,3,720]{3,2,1,0:T(4,128)}, /*ind...) while((s32[]{:T(128)}, f32[3,720]{1,0:T(4,128)S(1)}, ...), condition=%wide.region_4.5_spmd.clone.clone.clone.clone, body=%wide.region_3.4_spmd.clone.clone.clone.clone.sunk | while | flops 644713 | bytes 1742385 | solution.py:74
  63.7 0.8 fusion.92
  78.2 0.8 fusion.92
  92.7 0.8 fusion.92
  107.2 0.8 fusion.92
  121.7 0.8 fusion.92
  136.2 0.8 fusion.92
  150.7 0.8 fusion.92
  165.3 0.8 fusion.92
  179.8 0.8 fusion.92
  194.3 0.8 fusion.92
  208.8 0.8 fusion.92
  223.3 0.8 fusion.92
  237.8 0.8 fusion.92
  252.3 0.8 fusion.92
  266.9 0.8 fusion.92
  281.4 0.8 fusion.92
  295.9 0.8 fusion.92
  310.4 0.8 fusion.92
  324.9 0.8 fusion.92
  339.4 0.8 fusion.92
  353.9 0.8 fusion.92
  368.4 0.8 fusion.92
  382.9 0.8 fusion.92
  398.2 0.8 copy.92
  399.0 6.7 %all-to-all-start = ((bf16[1,1,90,16,90]{4,2,1,0,3:T(8,128)(2,1)}), bf16[1,1,90,16,90]{4,2,1,0,3:T(8,128)(2,1)S(1)}, u32[]{:S(2)}, u32[]{:S(2)}) async-start(bf16[1,1,90,16,90]{4,2,1,0,3:T(8,128)(2,1)} %copy.92), calls=%async_computation | async-start | bytes 786432 | tf_op jit(solution)/shard_map/all_to_all | solution.py:130
  405.7 6.2 %copy.105 = f32[384,3,720]{0,2,1:T(8,128)} copy(f32[384,3,720]{2,1,0:T(4,128)} %bitcast.574) | data formatting | bytes 6635520 | tf_op jit(solution)/shard_map/reshape | solution.py:74
  412.0 0.7 mul.2213
  412.8 3.4 fusion.61
  416.2 0.8 reshape.1512
  417.1 1.6 all-to-all-done
  418.6 1.0 convert_bitcast_fusion.1
  419.6 1.5 reshape.1525
  421.1 5.7 fusion.53
  426.9 3.2 reduce_sum.94
  431.4 6.1 %all-to-all-start.3 = ((bf16[8,3,2,1,1,90]{5,2,4,3,1,0:T(2,128)(2,1)}), bf16[8,3,2,1,1,90]{5,2,4,3,1,0:T(2,128)(2,1)S(1)}, u32[]{:S(2)}, u32[]{:S(2)}) async-start(bf16[8,3,2,1,1,90]{5,2,4,3,1,0:T(2,128)(2,1)} %copy.102), calls=%async_computation.4 | async-start | bytes 24576 | tf_op jit(solution)/shard_map/all_to_all | solution.py:168
  437.6 2.2 fusion.70
  439.8 6.7 %all-to-all-done.3 = bf16[8,3,2,1,1,90]{5,2,4,3,1,0:T(2,128)(2,1)S(1)} async-done(((bf16[8,3,2,1,1,90]{5,2,4,3,1,0:T(2,128)(2,1)}), bf16[8,3,2,1,1,90]{5,2,4,3,1,0:T(2,128)(2,1)S(1)}, u32[]{:S(2)}, u32[]{:S(2)}) %all-to-all-start.3) | async-done | bytes 8672 | tf_op jit(solution)/shard_map/all_to_all | solution.py:168
  446.5 5.4 all-to-all-start.1
  452.7 1.0 reshape.1515
  453.7 1.8 fusion.78
  456.2 13.7 %while.42 = (s32[]{:T(128)}, f32[3]{0:T(128)S(1)}, bf16[3,2,1,16,384]{4,3,1,2,0:T(8,128)(2,1)}, f32[3]{0:T(128)S(1)}, f32[3,2,1,17,384]{4,3,1,2,0:T(8,128)}, /*index=5*/s32[]{:T(128)}) while((s32[]{:T(128)}, f32[3]{0:T(128)S(1)}, bf16[3,2,1,16,384]{4,3,1,2,0:T(8,128)(2,1)}, f32[3]{0:T(128)S(1)}, f32[3,2,1,17,384]{4,3,1,2,0:T(8,128)}, ...), condition=%wide.region_10.11_spmd, body=%wide.region_5.10_spmd.sunk | while | flops 1372417 | bytes 3005033 | solution.py:190
  456.2 0.9 dynamic-slice_bitcast_fusion.2
  458.0 1.3 select_reduce_fusion.3
  460.8 0.9 dynamic-slice_bitcast_fusion.2
  462.6 1.3 select_reduce_fusion.3
  465.4 0.9 dynamic-slice_bitcast_fusion.2
  467.2 1.3 select_reduce_fusion.3
  470.0 2.1 convolution_convert_fusion.1
  472.3 0.9 copy.107
  473.2 9.7 %all-to-all-start.4 = ((bf16[1,3,2,1,128,90]{5,2,1,3,0,4:T(2,128)(2,1)}), bf16[1,3,2,1,128,90]{5,2,1,3,0,4:T(2,128)(2,1)S(1)}, u32[]{:S(2)}, u32[]{:S(2)}) async-start(bf16[1,3,2,1,128,90]{5,2,1,3,0,4:T(2,128)(2,1)} %copy.107), calls=%async_computation.5 | async-start | bytes 393216 | tf_op jit(solution)/shard_map/all_to_all | solution.py:202
  482.9 0.9 fusion.64
  486.3 79.1 %psum.7 = f32[]{:T(128)} all-reduce(f32[]{:T(128)S(6)} %add.767), channel_id=1, replica_groups=mesh['chan'=2,'ens'=16,'lat'=8] {'chan','ens','lat'}, use_global_device_ids=true, to_apply=%region_14.15 | all-reduce | flops 1 | bytes 8 | tf_op jit(solution)/shard_map/psum | solution.py:212
  565.9 1.1 reshape.1526
  567.1 1.6 fusion.54
  568.7 1.4 copy.108
  (1302 shorter events, 89.7 us)
Async XLA Ops:
  7.2 422.9 %reduce-scatter.2.cloned.1.call-start = ((), (), s32[]{:S(2)}) async-start(), calls=%async_computation.6 | async-start | bytes 417792 | tf_op jit(solution)/shard_map/reduce_scatter | solution.py:124
  24.4 5.2 copy-start.4
  29.4 1.4 copy-start
  32.5 366.6 %all-to-all-start.2 = ((bf16[128,3,2,1,1,90]{5,2,1,4,3,0:T(2,128)(2,1)}), bf16[128,3,2,1,1,90]{5,2,1,4,3,0:T(2,128)(2,1)S(1)}, u32[]{:S(2)}, u32[]{:S(2)}) async-start(bf16[128,3,2,1,1,90]{5,2,1,4,3,0:T(2,128)(2,1)} %bitcast.19), calls=%async_computation.2 | async-start | bytes 393216 | tf_op jit(solution)/shard_map/all_to_all | solution.py:166
  399.0 38.5 %copy-start.2 = (f32[90,90]{1,0:T(8,128)}, f32[90,90]{1,0:T(8,128)S(1)}, u32[]{:S(2)}) copy-start(f32[90,90]{1,0:T(8,128)S(1)} %bitcast_convert_fusion) | copy-start | bytes 97204
  399.0 19.6 %all-to-all-start = ((bf16[1,1,90,16,90]{4,2,1,0,3:T(8,128)(2,1)}), bf16[1,1,90,16,90]{4,2,1,0,3:T(8,128)(2,1)S(1)}, u32[]{:S(2)}, u32[]{:S(2)}) async-start(bf16[1,1,90,16,90]{4,2,1,0,3:T(8,128)(2,1)} %copy.92), calls=%async_computation | async-start | bytes 786432 | tf_op jit(solution)/shard_map/all_to_all | solution.py:130
  426.9 25.1 %copy-start.1 = (bf16[3,2,1,16,720]{4,3,1,0,2:T(8,128)(2,1)S(1)}, bf16[3,2,1,16,720]{4,3,1,0,2:T(8,128)(2,1)}, u32[]{:S(2)}) copy-start(bf16[3,2,1,16,720]{4,3,1,0,2:T(8,128)(2,1)} %reshape.1512) | copy-start | bytes 414724
  431.4 15.1 %all-to-all-start.3 = ((bf16[8,3,2,1,1,90]{5,2,4,3,1,0:T(2,128)(2,1)}), bf16[8,3,2,1,1,90]{5,2,4,3,1,0:T(2,128)(2,1)S(1)}, u32[]{:S(2)}, u32[]{:S(2)}) async-start(bf16[8,3,2,1,1,90]{5,2,4,3,1,0:T(2,128)(2,1)} %copy.102), calls=%async_computation.4 | async-start | bytes 24576 | tf_op jit(solution)/shard_map/all_to_all | solution.py:168
  446.5 26.7 %all-to-all-start.1 = ((bf16[1,16,90,1,90]{4,2,3,0,1:T(8,128)(2,1)}), bf16[1,16,90,1,90]{4,2,3,0,1:T(8,128)(2,1)S(1)}, u32[]{:S(2)}, u32[]{:S(2)}) async-start(bf16[1,16,90,1,90]{4,2,3,0,1:T(8,128)(2,1)} %fusion.70), calls=%async_computation.1 | async-start | bytes 786432 | tf_op jit(solution)/shard_map/all_to_all | solution.py:156
  470.0 12.9 %copy-start.3 = (f32[90,90]{1,0:T(8,128)S(1)}, f32[90,90]{1,0:T(8,128)}, u32[]{:S(2)}) copy-start(f32[90,90]{1,0:T(8,128)} %copy-done.2) | copy-start | bytes 97204
  473.2 93.9 %all-to-all-start.4 = ((bf16[1,3,2,1,128,90]{5,2,1,3,0,4:T(2,128)(2,1)}), bf16[1,3,2,1,128,90]{5,2,1,3,0,4:T(2,128)(2,1)S(1)}, u32[]{:S(2)}, u32[]{:S(2)}) async-start(bf16[1,3,2,1,128,90]{5,2,1,3,0,4:T(2,128)(2,1)} %copy.107), calls=%async_computation.5 | async-start | bytes 393216 | tf_op jit(solution)/shard_map/all_to_all | solution.py:202
Sparse Core Ops, SparseCore 0:
  30.9 78.3 reduce-scatter.1
where the time goes:
time: 582 us; the launch traced here: 577 us
  loops' own time  254 us (44%)
  other arithmetic  93.7 us (16%)
  blocking collectives  79.1 us (14%)
  local copies, waits for them, and re-layouts  74.8 us (13%)
  starting transfers between devices  44.2 us (8%)
  between operations  16.3 us (3%)
  waiting for transfers between devices  8.35 us (1%)
  matrix products  6.56 us (1%)
    another operation x1, loops' own time, legendre_table(): lax.scan(recur, initial, jnp.arange(DEGREE_CUTOFF, dtype=jnp.int32), unro...  254 us
    psum x1, blocking collectives, local(): ensemble_loss = lax.psum(local_total, ('chan', 'ens', 'lat'))  79.1 us
    while x360, other arithmetic  41.5 us
    slice x24, local copies, waits for them, and re-layouts, legendre_table(): lax.scan(recur, initial, jnp.arange(DEGREE_CUTOFF, dtype=jnp.int32), unro...  18.4 us
    dynamic_update_slice x24, local copies, waits for them, and re-layouts, legendre_table(): lax.scan(recur, initial, jnp.arange(DEGREE_CUTOFF, dtype=jnp.int32), unro...  17.2 us
    all_to_all x1, starting transfers between devices, local(): lax.all_to_all(outgoing, ('ens', 'lat'), split_axis=0, concat_axis=4, til...  16.3 us
  transfers between devices with their start and end apart: 6, of which 2 were waited for; matrix products, arithmetic and copies ran while one was open for 26% of the time, Pallas kernels for 0%

commit v1 on v0

v1 whole, which is shorter than its diff:
```python
import functools
import math

import jax
import jax.numpy as jnp
from jax import lax
from jax.experimental import pallas as pl
from jax.experimental.pallas import tpu as pltpu
from jax.sharding import PartitionSpec as P

PARALLEL_LINES = 720
AZIMUTH_STEPS = 1440
DEGREE_CUTOFF = 384
SOFTENING_EPS = 0.25
SPECTRAL_WEIGHT = 0.1

MEMBERS = 16
BANDS = 8
GROUPS = MEMBERS * BANDS
ORDERS = DEGREE_CUTOFF // GROUPS
BAND_ROWS = PARALLEL_LINES // BANDS
LON_BLOCK = AZIMUTH_STEPS // MEMBERS
ROW_GROUPS = 15
GROUP_ROWS = 6
LANES = 128
LON_CHUNKS = 12
LON_PADDED = LON_CHUNKS * LANES
SPECTRAL_ROWS = GROUPS * 8
BLOCK = 16

VMEM = pltpu.VMEM
F32 = jnp.float32
BF16 = jnp.bfloat16


def params(**kw):
    return pltpu.CompilerParams(vmem_limit_bytes=48 << 20, **kw)


def iota(shape, dim):
    return lax.broadcasted_iota(jnp.int32, shape, dim)


def cos_sin(steps):
    quarter = jnp.floor(steps * (1.0 / 360.0) + 0.5)
    rest = (steps - 360.0 * quarter) * (2.0 * math.pi / AZIMUTH_STEPS)
    quadrant = quarter - 4.0 * jnp.floor(quarter * 0.25)
    square = rest * rest
    sine = rest * (
        1.0
        + square
        * (-1.0 / 6.0 + square * (1.0 / 120.0 + square * (-1.0 / 5040.0 + square * (1.0 / 362880.0))))
    )
    cosine = 1.0 + square * (
        -0.5
        + square
        * (1.0 / 24.0 + square * (-1.0 / 720.0 + square * (1.0 / 40320.0 - square * (1.0 / 3628800.0))))
    )
    odd = (quadrant == 1.0) | (quadrant == 3.0)
    cos_part = jnp.where(odd, sine, cosine)
    sin_part = jnp.where(odd, cosine, sine)
    cos_part = jnp.where((quadrant == 1.0) | (quadrant == 2.0), -cos_part, cos_part)
    sin_part = jnp.where(quadrant >= 2.0, -sin_part, sin_part)
    return cos_part, sin_part


def dft_kernel(out_ref):
    def body(block, carry):
        row = block * BLOCK + iota((BLOCK, LANES), 0)
        lane = iota((BLOCK, LANES), 1)
        part = row & 7
        order = (ORDERS * (row >> 3) + (part >> 1)).astype(F32)
        turn = (360 * (part & 1)).astype(F32)
        cosine, sine = cos_sin(order * lane.astype(F32) + turn)
        cosine = jnp.where(part < 2 * ORDERS, cosine, 0.0)
        sine = jnp.where(part < 2 * ORDERS, sine, 0.0)
        cos_step, sin_step = cos_sin(order * float(LANES))
        rows = pl.ds(pl.multiple_of(block * BLOCK, BLOCK), BLOCK)
        for chunk in range(LON_CHUNKS):
            value = cosine
            if chunk == LON_CHUNKS - 1:
                value = jnp.where(lane < AZIMUTH_STEPS - LANES * chunk, value, 0.0)
            out_ref[rows, LANES * chunk : LANES * (chunk + 1)] = value.astype(BF16)
            cosine, sine = (
                cosine * cos_step - sine * sin_step,
                sine * cos_step + cosine * sin_step,
            )
        return carry

    lax.fori_loop(0, SPECTRAL_ROWS // BLOCK, body, 0)


def dft_table():
    return pl.pallas_call(
        dft_kernel,
        out_shape=jax.ShapeDtypeStruct((SPECTRAL_ROWS, LON_PADDED), BF16),
        out_specs=pl.BlockSpec(memory_space=VMEM),
        compiler_params=params(),
        cost_estimate=pl.CostEstimate(flops=20_000_000, bytes_accessed=3 << 20, transcendentals=0),
    )()


def lat_rows(rows_index):
    colatitude = math.pi * (rows_index.astype(F32) + 0.5) / PARALLEL_LINES
    return (jnp.cos(colatitude), jnp.sin(colatitude))


def seed_log(order_values):
    factors = jnp.arange(1, DEGREE_CUTOFF + 1, dtype=jnp.int32).astype(F32)[None, :]
    summands = jnp.where(factors <= order_values[:, None], jnp.log1p(-0.5 / factors), 0.0)
    return 0.5 * jnp.log(order_values + 0.5) + 0.5 * jnp.sum(summands, axis=1)


def recurrence(order_values):
    degree = jnp.arange(DEGREE_CUTOFF, dtype=jnp.int32).astype(F32)[None, :]
    order = order_values[:, None]
    growing = degree > order
    denominator = jnp.where(growing, degree * degree - order * order, 1.0)
    leading = jnp.sqrt(jnp.maximum(4.0 * degree * degree - 1.0, 0.0) / denominator)
    trailing = jnp.sqrt(
        jnp.maximum(
            ((degree - 1.0) ** 2 - order * order)
            * (2.0 * degree + 1.0)
            / ((2.0 * degree - 3.0) * denominator),
            0.0,
        )
    )
    zero = jnp.zeros_like(leading)
    return jnp.concatenate(
        [
            jnp.where(growing, leading, zero),
            jnp.where(growing, trailing, zero),
            (degree == order).astype(F32),
        ],
        axis=0,
    )


def legendre_kernel(coef_ref, cos_ref, weight_ref, start_ref, out_ref, table_ref):
    cos_lat = cos_ref[...]
    weight = weight_ref[...]

    def body(block, carry):
        state = list(carry)
        for step in range(BLOCK):
            degree = block * BLOCK + step
            for index in range(ORDERS):
                latest, before, log_scale, factor = state[4 * index : 4 * index + 4]
                leading = coef_ref[index, degree]
                trailing = coef_ref[ORDERS + index, degree]
                begin = coef_ref[2 * ORDERS + index, degree]
                advanced = (leading * cos_lat) * latest + (begin - trailing * before)
                row = (index * DEGREE_CUTOFF + degree) * 8
                table_ref[pl.ds(pl.multiple_of(row, 8), 8), :] = advanced * factor
                state[4 * index : 4 * index + 4] = [advanced, latest, log_scale, factor]
        for index in range(ORDERS):
            latest, before, log_scale, factor = state[4 * index : 4 * index + 4]
            largest = jnp.maximum(jnp.abs(latest), jnp.abs(before))
            largest = jnp.where(largest > 0.0, largest, 1.0)
            shrink = 1.0 / largest
            log_scale = log_scale + jnp.log(largest)
            state[4 * index : 4 * index + 4] = [
                latest * shrink,
                before * shrink,
                log_scale,
                jnp.exp(log_scale) * weight,
            ]
        return tuple(state)

    state = []
    for index in range(ORDERS):
        start = start_ref[8 * index : 8 * index + 8, :]
        state += [jnp.zeros((8, LANES), F32), jnp.zeros((8, LANES), F32), start, jnp.exp(start) * weight]
    lax.fori_loop(0, DEGREE_CUTOFF // BLOCK, body, tuple(state))
    for index in range(ORDERS):
        for band in range(BANDS):
            rows = table_ref[pl.ds(index * DEGREE_CUTOFF * 8 + band, DEGREE_CUTOFF, stride=8), :]
            out_ref[index, :, LANES * band : LANES * (band + 1)] = rows.astype(BF16)


def legendre_table(order_values):
    lane = jnp.arange(LANES, dtype=jnp.int32)[None, :]
    band = jnp.arange(BANDS, dtype=jnp.int32)[:, None]
    valid = ((lane >> 3) < ROW_GROUPS) & ((lane & 7) < GROUP_ROWS)
    row = jnp.where(valid, BAND_ROWS * band + GROUP_ROWS * (lane >> 3) + (lane & 7), 0)
    cos_lat, sin_lat = lat_rows(row)
    weight = jnp.where(valid, math.pi / PARALLEL_LINES * sin_lat, 0.0)
    start = seed_log(order_values)[:, None, None] + order_values[:, None, None] * jnp.log(sin_lat)[None]
    return pl.pallas_call(
        legendre_kernel,
        out_shape=jax.ShapeDtypeStruct((ORDERS, DEGREE_CUTOFF, BANDS * LANES), BF16),
        in_specs=[pl.BlockSpec(memory_space=pltpu.SMEM)] + [pl.BlockSpec(memory_space=VMEM)] * 3,
        out_specs=pl.BlockSpec(memory_space=VMEM),
        scratch_shapes=[VMEM((ORDERS * DEGREE_CUTOFF * 8, LANES), F32)],
        compiler_params=params(),
        cost_estimate=pl.CostEstimate(flops=20_000_000, bytes_accessed=3 << 20, transcendentals=0),
    )(recurrence(order_values), cos_lat, weight, start.reshape(8 * ORDERS, LANES))


def truth_rows(message_ref):
    lane = iota((8, LANES), 1)
    base = AZIMUTH_STEPS - (LON_CHUNKS - 1) * LANES
    chunks = [jnp.zeros((8, LANES), F32) for _ in range(LON_CHUNKS)]
    for pair in range(MEMBERS // 2):
        both = message_ref[16 * pair : 16 * pair + 16, LON_PADDED - LANES :].astype(F32)
        for half in range(2):
            first = LON_BLOCK * (2 * pair + half)
            value = both[8 * half : 8 * half + 8]
            shift = (first - base) % LANES
            if shift:
                value = pltpu.roll(value, shift, 1)
            for chunk in range(first // LANES, (first + LON_BLOCK - 1) // LANES + 1):
                place = lane + chunk * LANES
                inside = (place >= first) & (place < first + LON_BLOCK)
                chunks[chunk] = jnp.where(inside, value, chunks[chunk])
    return chunks


def fourier_kernel(table_ref, own_ref, message_ref, out_ref, field_ref):
    field_ref[0:112, :] = own_ref[0:112, :]
    truth = truth_rows(message_ref)
    for chunk in range(LON_CHUNKS):
        lanes = slice(LANES * chunk, LANES * (chunk + 1))
        last = own_ref[112:128, lanes].astype(F32)[0:8]
        field_ref[112:128, lanes] = jnp.concatenate([last, truth[chunk]], axis=0).astype(BF16)
    for block in range(4):
        rows = slice(256 * block, 256 * (block + 1))
        out_ref[rows, :] = lax.dot_general(
            table_ref[rows, :],
            field_ref[...],
            (((1,), (1,)), ((), ())),
            preferred_element_type=F32,
        ).astype(BF16)


def fourier(table, own, message):
    return pl.pallas_call(
        fourier_kernel,
        out_shape=jax.ShapeDtypeStruct((SPECTRAL_ROWS, LANES), BF16),
        in_specs=[pl.BlockSpec(memory_space=VMEM)] * 3,
        out_specs=pl.BlockSpec(memory_space=VMEM),
        scratch_shapes=[VMEM((LANES, LON_PADDED), BF16)],
        compiler_params=params(),
        cost_estimate=pl.CostEstimate(flops=400_000_000, bytes_accessed=4 << 20, transcendentals=0),
    )(table, own, message)


def grid_kernel(message_ref, weight_ref, out_ref, loss_ref, truth_ref):
    for chunk, value in enumerate(truth_rows(message_ref)):
        truth_ref[:, LANES * chunk : LANES * (chunk + 1)] = value
    weight = weight_ref[...]
    lane = iota((8, LANES), 1)

    def body(chunk, total):
        lanes = pl.ds(pl.multiple_of(chunk * LANES, LANES), LANES)
        draws = []
        for pair in range(MEMBERS // 2):
            both = message_ref[16 * pair : 16 * pair + 16, lanes].astype(F32)
            draws += [both[0:8], both[8:16]]
        target = truth_ref[:, lanes]
        counts = [None] * MEMBERS
        for i in range(MEMBERS):
            for k in range(i + 1, MEMBERS):
                above = jnp.where(draws[i] > draws[k], 1.0, 0.0)
                turn = jnp.where(draws[i] < draws[k], -1.0, above)
                counts[i] = turn if counts[i] is None else counts[i] + turn
                counts[k] = -turn if counts[k] is None else counts[k] - turn
        spread = jnp.zeros((8, LANES), F32)
        pulls = []
        for i in range(MEMBERS):
            gap = draws[i] - target
            above = jnp.where(draws[i] > target, float(MEMBERS - 1), 0.0)
            side = jnp.where(draws[i] < target, -float(MEMBERS - 1), above)
            pulls.append(side - counts[i])
            spread = spread + (jnp.abs(gap) - (draws[i] * counts[i]) * (1.0 / (MEMBERS - 1)))
        for pair in range(MEMBERS // 2):
            both = jnp.concatenate([pulls[2 * pair], pulls[2 * pair + 1]], axis=0)
            out_ref[16 * pair : 16 * pair + 16, lanes] = both.astype(BF16)
        return total + jnp.where(lane + chunk * LANES < AZIMUTH_STEPS, spread, 0.0)

    total = lax.fori_loop(0, LON_CHUNKS, body, jnp.zeros((8, LANES), F32))
    loss_ref[...] = total * weight


def grid_counts(message, weight):
    return pl.pallas_call(
        grid_kernel,
        out_shape=(
            jax.ShapeDtypeStruct((LANES, LON_PADDED), BF16),
            jax.ShapeDtypeStruct((8, LANES), F32),
        ),
        in_specs=[pl.BlockSpec(memory_space=VMEM)] * 2,
        out_specs=(pl.BlockSpec(memory_space=VMEM), pl.BlockSpec(memory_space=VMEM)),
        scratch_shapes=[VMEM((8, LON_PADDED), F32)],
        compiler_params=params(),
        cost_estimate=pl.CostEstimate(flops=40_000_000, bytes_accessed=1 << 20, transcendentals=0),
    )(message, weight)


def spectral_kernel(first_ref, modes_ref, table_ref, grid_ref, out_ref, wide_ref, lhs_ref):
    draws = MEMBERS
    scale = SPECTRAL_WEIGHT * PARALLEL_LINES * AZIMUTH_STEPS / (DEGREE_CUTOFF * (DEGREE_CUTOFF + 1) / 2)
    lane = iota((64, LANES), 1)
    target = jnp.zeros((64, LANES), F32)
    for member in range(draws):
        value = modes_ref[64 * member : 64 * member + 64, :].astype(F32)
        wide_ref[64 * member : 64 * member + 64, :] = value
        if member < ROW_GROUPS:
            moved = pltpu.roll(value, (8 * member + 8) % LANES, 1)
            target = jnp.where((lane >> 3) == member, moved, target)
    loss = jnp.zeros((1, DEGREE_CUTOFF), F32)
    degree = iota((1, DEGREE_CUTOFF), 1)
    pad = jnp.zeros((14, LANES), F32)
    grads = []
    for index in range(ORDERS):
        for band in range(BANDS):
            lanes = slice(LANES * band, LANES * (band + 1))
            parts = [
                wide_ref[pl.ds(8 * band + 2 * index + r, draws, stride=64), :] for r in range(2)
            ]
            aims = [target[8 * band + 2 * index + r : 8 * band + 2 * index + r + 1, :] for r in range(2)]
            lhs_ref[index, :, lanes] = jnp.concatenate(parts + aims + [pad], axis=0).astype(BF16)
        terms = lax.dot_general(
            lhs_ref[index],
            table_ref[index],
            (((1,), (1,)), ((), ())),
            preferred_element_type=F32,
        )
        real, imag = terms[0:draws], terms[draws : 2 * draws]
        real_aim, imag_aim = terms[2 * draws : 2 * draws + 1], terms[2 * draws + 1 : 2 * draws + 2]
        gap_real, gap_imag = real - real_aim, imag - imag_aim
        square = gap_real * gap_real + gap_imag * gap_imag + SOFTENING_EPS**2
        inverse = lax.rsqrt(square)
        near = square * inverse
        step_real, step_imag = gap_real * inverse, gap_imag * inverse
        pair = jnp.zeros_like(real)
        pull_real, pull_imag = jnp.zeros_like(real), jnp.zeros_like(real)
        for other in range(draws):
            gap_real, gap_imag = real - real[other : other + 1], imag - imag[other : other + 1]
            square = gap_real * gap_real + gap_imag * gap_imag + SOFTENING_EPS**2
            inverse = lax.rsqrt(square)
            pair = pair + square * inverse
            pull_real = pull_real + gap_real * inverse
            pull_imag = pull_imag + gap_imag * inverse
        kept = degree >= first_ref[0] + index
        score = jnp.sum(near, axis=0, keepdims=True) - (
            jnp.sum(pair, axis=0, keepdims=True) - draws * SOFTENING_EPS
        ) / (2.0 * (draws - 1))
        loss = loss + jnp.where(kept, score, 0.0)
        down = jnp.concatenate(
            [step_real - pull_real / (draws - 1), step_imag - pull_imag / (draws - 1)], axis=0
        )
        grad = jnp.where(kept, scale * down, 0.0).astype(BF16)
        back = jnp.dot(grad, table_ref[index], preferred_element_type=F32)
        for band in range(BANDS):
            for r in range(2):
                wide_ref[pl.ds(8 * band + 2 * index + r, draws, stride=64), :] = back[
                    draws * r : draws * (r + 1), LANES * band : LANES * (band + 1)
                ]
    local = jnp.sum(jnp.sum(grid_ref[...], axis=0, keepdims=True), axis=1, keepdims=True) / (
        PARALLEL_LINES * AZIMUTH_STEPS
    ) + SPECTRAL_WEIGHT / (DEGREE_CUTOFF * (DEGREE_CUTOFF + 1) / 2) * jnp.sum(loss, axis=1, keepdims=True)
    high = local.astype(BF16).astype(F32)
    middle = (local - high).astype(BF16).astype(F32)
    low = local - high - middle
    row = iota((BLOCK, LANES), 0) & 7
    column = iota((BLOCK, LANES), 1)
    spare = jnp.where(column == LANES - 8, high, jnp.where(column == LANES - 7, middle, low))
    carries = (row == 0) & (column >= LANES - 8) & (column < LANES - 5)
    for block in range(SPECTRAL_ROWS // BLOCK):
        value = wide_ref[BLOCK * block : BLOCK * (block + 1), :]
        value = jnp.where(row < 2 * ORDERS, value, 0.0)
        out_ref[BLOCK * block : BLOCK * (block + 1), :] = jnp.where(carries, spare, value).astype(BF16)


def spectral(first, modes, table, grid_loss):
    return pl.pallas_call(
        spectral_kernel,
        out_shape=jax.ShapeDtypeStruct((SPECTRAL_ROWS, LANES), BF16),
        in_specs=[pl.BlockSpec(memory_space=pltpu.SMEM)] + [pl.BlockSpec(memory_space=VMEM)] * 3,
        out_specs=pl.BlockSpec(memory_space=VMEM),
        scratch_shapes=[
            VMEM((SPECTRAL_ROWS, LANES), F32),
            VMEM((ORDERS, 48, BANDS * LANES), BF16),
        ],
        compiler_params=params(),
        cost_estimate=pl.CostEstimate(flops=200_000_000, bytes_accessed=3 << 20, transcendentals=0),
    )(first, modes, table, grid_loss)


def final_kernel(table_ref, modes_ref, counts_ref, weight_ref, out_ref):
    for chunk in range(LON_CHUNKS):
        lanes = slice(LANES * chunk, LANES * (chunk + 1))
        width = min(LANES, AZIMUTH_STEPS - LANES * chunk)
        wave = lax.dot_general(
            modes_ref[...],
            table_ref[:, lanes],
            (((0,), (0,)), ((), ())),
            preferred_element_type=F32,
        )
        total = weight_ref[...] * counts_ref[:, lanes].astype(F32) + wave
        for group in range(ROW_GROUPS):
            out_ref[GROUP_ROWS * group : GROUP_ROWS * (group + 1), LANES * chunk : LANES * chunk + width] = total[
                8 * group : 8 * group + GROUP_ROWS, 0:width
            ]


def final(table, modes, counts, weight):
    return pl.pallas_call(
        final_kernel,
        out_shape=jax.ShapeDtypeStruct((BAND_ROWS, AZIMUTH_STEPS), F32),
        in_specs=[pl.BlockSpec(memory_space=VMEM)] * 4,
        out_specs=pl.BlockSpec(memory_space=VMEM),
        compiler_params=params(),
        cost_estimate=pl.CostEstimate(flops=400_000_000, bytes_accessed=4 << 20, transcendentals=0),
    )(table, modes, counts, weight)


def local(model_outputs, verifying_truth):
    ens_index = lax.axis_index("ens")
    lat_index = lax.axis_index("lat")
    own = model_outputs.reshape(ROW_GROUPS, GROUP_ROWS, AZIMUTH_STEPS)
    target = verifying_truth.reshape(ROW_GROUPS, GROUP_ROWS, LON_BLOCK)
    outgoing = jnp.concatenate([own, target], axis=2)
    outgoing = jnp.pad(
        outgoing,
        ((0, 1), (0, 8 - GROUP_ROWS), (0, LON_PADDED - AZIMUTH_STEPS - LON_BLOCK)),
    )
    message = lax.all_to_all(outgoing, "ens", split_axis=0, concat_axis=0, tiled=True)
    message = message.reshape(LANES, LON_PADDED)

    table = dft_table()
    first = ORDERS * (ens_index * BANDS + lat_index)
    orders = (first + jnp.arange(ORDERS, dtype=jnp.int32)).astype(F32)
    legendre = legendre_table(orders)

    modes = fourier(table, outgoing.reshape(LANES, LON_PADDED), message)
    modes = lax.all_to_all(
        modes.reshape(GROUPS, 8, LANES), ("ens", "lat"), split_axis=0, concat_axis=0, tiled=True
    ).reshape(SPECTRAL_ROWS, LANES)

    part = jnp.arange(8, dtype=jnp.int32)
    grid_row = BAND_ROWS * lat_index + GROUP_ROWS * ens_index + part
    grid_valid = (part < GROUP_ROWS) & (ens_index < ROW_GROUPS)
    grid_weight = jnp.where(grid_valid, lat_rows(grid_row)[1], 0.0)
    counts, grid_loss = grid_counts(message, jnp.broadcast_to(grid_weight[:, None], (8, LANES)))
    counts = lax.all_to_all(
        counts.reshape(MEMBERS, 8, LON_PADDED), "ens", split_axis=0, concat_axis=0, tiled=True
    ).reshape(LANES, LON_PADDED)

    back = spectral(first.reshape(1).astype(jnp.int32), modes, legendre, grid_loss)
    back = lax.all_to_all(
        back.reshape(GROUPS, 8, LANES), ("ens", "lat"), split_axis=0, concat_axis=0, tiled=True
    )
    shared = jnp.sum(back[:, 0, LANES - 8 : LANES - 5].astype(F32))
    other = lax.ppermute(shared, "chan", [(0, 1), (1, 0)])

    row = jnp.arange(LANES, dtype=jnp.int32)
    band_row = BAND_ROWS * lat_index + GROUP_ROWS * (row >> 3) + (row & 7)
    weight = lat_rows(band_row)[1] / (MEMBERS - 1)
    weight = jnp.broadcast_to(weight[:, None], (LANES, LANES))
    slope = final(table, back.reshape(SPECTRAL_ROWS, LANES), counts, weight)
    return (slope[None, None], shared + other)


def solution(mesh):
    return jax.shard_map(
        local,
        mesh=mesh,
        in_specs=(P("ens", "chan", "lat", None), P("chan", "lat", "ens")),
        out_specs=(P("ens", "chan", "lat", None), P()),
        check_vma=False,
    )
```

time: 582 us -> 105 us (0.18)
  loops' own time: 254 us -> 0 us
  other arithmetic: 93.7 us -> 10.7 us
  blocking collectives: 79.1 us -> 0 us
  local copies, waits for them, and re-layouts: 74.8 us -> 9.21 us
  Pallas kernels: 0 us -> 17.7 us
  waiting for transfers between devices: 8.35 us -> 23.8 us
  between operations: 16.3 us -> 3.25 us
  matrix products: 6.56 us -> 0 us
    another operation x2 -> x0, loops' own time: 254 us -> none  [the longest x1 254 us: legendre_table(): lax.scan(recur, initial, jnp.arange(DEGREE_CUTOFF, dtype=jnp.int32), unro...]
    psum x1 -> x0, blocking collectives: 79.1 us -> none  [local(): ensemble_loss = lax.psum(local_total, ('chan', 'ens', 'lat'))]
    while x360 -> x0, other arithmetic: 41.5 us -> none
    dynamic_update_slice x27 -> x0, local copies, waits for them, and re-layouts: 19.4 us -> none  [the longest x24 17.2 us: legendre_table(): lax.scan(recur, initial, jnp.arange(DEGREE_CUTOFF, dtype=jnp.int32), unro...]
    slice x27 -> x0, local copies, waits for them, and re-layouts: 18.4 us -> none  [the longest x24 18.4 us: legendre_table(): lax.scan(recur, initial, jnp.arange(DEGREE_CUTOFF, dtype=jnp.int32), unro...]
    pallas_call x0 -> x6, Pallas kernels: none -> 17.7 us  [the longest x1 5.61 us: legendre_table(): pl.pallas_call(legendre_kernel, out_shape=jax.ShapeDtypeStruct((ORDERS, D...]
    all_to_all x5 -> x4, waiting for transfers between devices: 8.33 us -> 22.9 us  [the longest x1 10.9 us: local(): lax.all_to_all(back.reshape(GROUPS, 8, LANES), ('ens', 'lat'), split_axis...]
    convert_element_type x6 -> x0, local copies, waits for them, and re-layouts: 13.8 us -> none  [the longest x2 9.9 us: dft_table(): stacked.reshape(AZIMUTH_STEPS, 2 * DEGREE_CUTOFF).astype(jnp.bfloat16)]
  transfers between devices with their start and end apart: 6 -> 5, of which waited for: 2 -> 4; matrix products, arithmetic and copies ran while one was open for 26% -> 10% of each run, Pallas kernels for 0% -> 14%
where the time goes in v1:
time: 105 us; the launch traced here: 104 us
  starting transfers between devices  39.6 us (38%)
  waiting for transfers between devices  23.8 us (23%)
  Pallas kernels  17.7 us (17%)
  other arithmetic  10.7 us (10%)
  local copies, waits for them, and re-layouts  9.21 us (9%)
  between operations  3.25 us (3%)
    all_to_all x1, starting transfers between devices, local(): lax.all_to_all(modes.reshape(GROUPS, 8, LANES), ('ens', 'lat'), split_axi...  11 us
    all_to_all x1, waiting for transfers between devices, local(): lax.all_to_all(back.reshape(GROUPS, 8, LANES), ('ens', 'lat'), split_axis...  10.9 us
    all_to_all x1, starting transfers between devices, local(): lax.all_to_all(back.reshape(GROUPS, 8, LANES), ('ens', 'lat'), split_axis...  10.5 us
    all_to_all x1, starting transfers between devices, local(): lax.all_to_all(outgoing, 'ens', split_axis=0, concat_axis=0, tiled=True)  9.17 us
    all_to_all x1, waiting for transfers between devices, local(): lax.all_to_all(modes.reshape(GROUPS, 8, LANES), ('ens', 'lat'), split_axi...  7.16 us
    pallas_call x1, Pallas kernels, legendre_table(): pl.pallas_call(legendre_kernel, out_shape=jax.ShapeDtypeStruct((ORDERS, D...  5.61 us
    ppermute x1, starting transfers between devices, local(): other = lax.ppermute(shared, 'chan', [(0, 1), (1, 0)])  5.09 us
    all_to_all x1, waiting for transfers between devices, local(): lax.all_to_all(outgoing, 'ens', split_axis=0, concat_axis=0, tiled=True)  4.77 us
  transfers between devices with their start and end apart: 5, of which 4 were waited for; matrix products, arithmetic and copies ran while one was open for 10% of the time, Pallas kernels for 14%

profile of v1, /device:TPU:1, one launch (start us, length us, event | category | flops | bytes accessed | tf_op | source)
XLA Modules:
  0.0 104.3 jit_solution(16280633751409660814)
XLA Ops:
  0.6 0.8 reshape.223
  1.4 0.0 copy-start.6
  1.4 1.1 %reshape.222 = bf16[15,6,1440]{2,1,0:T(8,128)(2,1)S(1)} reshape(bf16[1,1,90,1440]{3,2,1,0:T(8,128)(2,1)} %param.2) | data formatting | bytes 518400 | tf_op jit(solution)/shard_map/reshape | solution.py:422
  2.5 0.0 copy-start.4
  2.5 0.9 fusion.7
  3.4 9.2 %all-to-all-start = ((bf16[16,8,1536]{2,1,0:T(8,128)(2,1)}), bf16[16,8,1536]{2,1,0:T(8,128)(2,1)S(1)}, u32[]{:S(2)}, u32[]{:S(2)}) async-start(bf16[16,8,1536]{2,1,0:T(8,128)(2,1)} %fusion.7), calls=%async_computation | async-start | bytes 786432 | tf_op jit(solution)/shard_map/all_to_all | solution.py:429
  12.6 0.6 add_convert_fusion.1
  13.2 0.5 fusion.21
  13.7 0.6 iota_multiply_fusion
  14.3 0.0 copy-done.6
  14.3 0.0 copy-done.4
  14.3 0.0 copy-start.8
  14.3 0.0 copy-start.9
  14.3 0.0 copy-start.5
  14.3 0.0 copy-start.7
  14.3 4.2 %shard_map.41.table_ref = bf16[1024,1536]{1,0:T(8,128)(2,1)S(1)} custom-call(), custom_call_target="tpu_custom_call" | custom-call | flops 20000000 | bytes 3145728 | tf_op jit(solution)/shard_map/pallas_call | solution.py:94
  18.5 0.0 copy-done.8
  18.5 0.0 copy-done.9
  18.5 1.3 %compare_select_fusion.1 = (f32[3,384]{1,0:T(4,128)}, f32[3,384]{1,0:T(4,128)}, f32[3]{0:T(128)}) fusion(f32[3]{0:T(128)S(1)} %copy-done.9, f32[384]{0:T(512)S(1)} %get-tuple-element.21, f32[384]{0:T(512)S(1)} %get-tuple-element.16, f32[384]{0:T(512)S(1)} %get-tuple-element.19, f32[3]{0:T(128)S(1)} %copy-done.8, f32[384]{0:T(512)S(1)} %get-tuple-element.22, ...), kind=kLoop, calls=%fused_computation.18 | loop fusion | flops 16125 | bytes 21540 | tf_op jit(solution)/shard_map/jit(_where)/select_n | solution.py:131
  19.9 0.0 copy-done.5
  19.9 0.0 copy-done.7
  19.9 0.0 copy-start.10
  19.9 0.9 fusion.22.own_ref
  20.8 4.8 %all-to-all-done = bf16[16,8,1536]{2,1,0:T(8,128)(2,1)S(1)} async-done(((bf16[16,8,1536]{2,1,0:T(8,128)(2,1)}), bf16[16,8,1536]{2,1,0:T(8,128)(2,1)S(1)}, u32[]{:S(2)}, u32[]{:S(2)}) %all-to-all-start) | async-done | bytes 393248 | tf_op jit(solution)/shard_map/all_to_all | solution.py:429
  25.6 0.0 copy-start
  25.6 1.0 copy-done
  26.6 1.0 shard_map.42
  27.6 0.0 copy-start.1
  27.6 0.7 copy-done.1
  28.3 11.0 %all-to-all-start.1 = ((bf16[128,8,128]{2,1,0:T(8,128)(2,1)}), bf16[128,8,128]{2,1,0:T(8,128)(2,1)}, u32[]{:S(2)}, u32[]{:S(2)}) async-start(bf16[128,8,128]{2,1,0:T(8,128)(2,1)} %bitcast.19), calls=%async_computation.1 | async-start | bytes 524288 | tf_op jit(solution)/shard_map/all_to_all | solution.py:438
  39.4 0.0 copy-done.10
  39.4 0.6 add_multiply_fusion.2
  39.9 0.7 compare_convert_fusion
  40.7 0.1 broadcast_in_dim.74.weight_ref
  40.7 1.6 %shard_map.44 = (bf16[128,1536]{1,0:T(8,128)(2,1)S(1)}, f32[8,128]{1,0:T(8,128)S(1)}) custom-call(bf16[128,1536]{1,0:T(8,128)(2,1)S(1)} %bitcast.16, f32[8,128]{1,0:T(8,128)S(1)} %broadcast_in_dim.74.weight_ref), custom_call_target="tpu_custom_call" | custom-call | flops 40000000 | bytes 1048576 | tf_op jit(solution)/shard_map/pallas_call | solution.py:286
  42.4 0.0 copy-start.3
  42.4 0.7 copy-done.3
  43.1 7.2 %all-to-all-done.1 = bf16[128,8,128]{2,1,0:T(8,128)(2,1)} async-done(((bf16[128,8,128]{2,1,0:T(8,128)(2,1)}), bf16[128,8,128]{2,1,0:T(8,128)(2,1)}, u32[]{:S(2)}, u32[]{:S(2)}) %all-to-all-start.1) | async-done | bytes 262176 | tf_op jit(solution)/shard_map/all_to_all | solution.py:438
  50.3 3.8 %all-to-all-start.3 = ((bf16[16,8,1536]{2,1,0:T(8,128)(2,1)}), bf16[16,8,1536]{2,1,0:T(8,128)(2,1)S(1)}, u32[]{:S(2)}, u32[]{:S(2)}) async-start(bf16[16,8,1536]{2,1,0:T(8,128)(2,1)} %bitcast.21), calls=%async_computation.3 | async-start | bytes 786432 | tf_op jit(solution)/shard_map/all_to_all | solution.py:447
  54.1 0.5 compare_and_fusion
  54.7 0.7 mul.165
  55.4 0.6 mul.166
  56.0 0.7 add.222
  56.7 0.6 add.223
  57.3 0.7 pad_maximum_fusion.coef_ref
  58.1 0.8 fusion.13
  58.8 0.7 fusion.10.start_ref
  59.6 5.6 %shard_map.43.table_ref = bf16[3,384,1024]{2,1,0:T(8,128)(2,1)S(1)} custom-call(f32[9,384]{1,0:T(8,128)S(1)} %pad_maximum_fusion.coef_ref, f32[8,128]{1,0:T(8,128)S(1)} %get-tuple-element.14.cos_ref, f32[8,128]{1,0:T(8,128)S(1)} %get-tuple-element.13.weight_ref, f32[24,128]{1,0:T(8,128)S(1)} %fusion.10.start_ref), custom_call_target="tpu_custom_call" | custom-call | flops 20000000 | bytes 3145728 | tf_op jit(solution)/shard_map/pallas_call | solution.py:189
  65.2 3.3 %shard_map.45 = bf16[1024,128]{1,0:T(8,128)(2,1)S(1)} custom-call(s32[1]{0:T(128)} %bitcast.first_ref, bf16[1024,128]{1,0:T(8,128)(2,1)} %bitcast.4.modes_ref, bf16[3,384,1024]{2,1,0:T(8,128)(2,1)S(1)} %shard_map.43.table_ref, f32[8,128]{1,0:T(8,128)S(1)} %get-tuple-element.4.grid_ref), custom_call_target="tpu_custom_call" | custom-call | flops 200000000 | bytes 3145728 | tf_op jit(solution)/shard_map/pallas_call | solution.py:377
  68.5 0.0 copy-start.2
  68.5 0.7 copy-done.2
  69.2 0.0 all-to-all-done.3
  69.2 10.5 %all-to-all-start.2 = ((bf16[128,8,128]{2,1,0:T(8,128)(2,1)}), bf16[128,8,128]{2,1,0:T(8,128)(2,1)}, u32[]{:S(2)}, u32[]{:S(2)}) async-start(bf16[128,8,128]{2,1,0:T(8,128)(2,1)} %bitcast.20), calls=%async_computation.2 | async-start | bytes 524288 | tf_op jit(solution)/shard_map/all_to_all | solution.py:452
  79.7 10.9 %all-to-all-done.2 = bf16[128,8,128]{2,1,0:T(8,128)(2,1)} async-done(((bf16[128,8,128]{2,1,0:T(8,128)(2,1)}), bf16[128,8,128]{2,1,0:T(8,128)(2,1)}, u32[]{:S(2)}, u32[]{:S(2)}) %all-to-all-start.2) | async-done | bytes 262176 | tf_op jit(solution)/shard_map/all_to_all | solution.py:452
  90.7 0.1 broadcast_in_dim.75.weight_ref
  90.7 2.0 %shard_map.46 = f32[90,1440]{1,0:T(8,128)S(1)} custom-call(bf16[1024,1536]{1,0:T(8,128)(2,1)S(1)} %shard_map.41.table_ref, bf16[1024,128]{1,0:T(8,128)(2,1)} %bitcast.7.modes_ref, bf16[128,1536]{1,0:T(8,128)(2,1)S(1)} %bitcast.18, f32[128,128]{1,0:T(8,128)S(1)} %broadcast_in_dim.75.weight_ref), custom_call_target="tpu_custom_call" | custom-call | flops 400000000 | bytes 4194304 | tf_op jit(solution)/shard_map/pallas_call | solution.py:409
  92.7 1.4 %copy.5 = f32[1,1,90,1440]{3,1,2,0:T(1,128)} copy(f32[1,1,90,1440]{3,2,1,0:T(8,128)S(1)} %bitcast.17) | data formatting | bytes 1036800
  94.1 1.8 %fusion.9 = f32[]{:T(128)} fusion(bf16[128,8,128]{2,1,0:T(8,128)(2,1)} %all-to-all-done.2), kind=kLoop, calls=%fused_computation.13 | loop fusion | flops 767 | bytes 772 | tf_op jit(solution)/shard_map/reduce_sum | solution.py:455
  95.9 5.1 %collective-permute-start = (f32[]{:T(128)}, f32[]{:T(128)}, u32[]{:S(2)}, u32[]{:S(2)}) collective-permute-start(f32[]{:T(128)} %fusion.9), channel_id=1, source_target_pairs={{0,128},{128,0},{1,129},{129,1},{2,130},{130,2},{3,131},{131,3},{4... | collective-permute-start | bytes 20 | tf_op jit(solution)/shard_map/ppermute | solution.py:456
  100.9 1.0 collective-permute-done
  (7 shorter events, 0.1 us)
Async XLA Ops:
  1.4 12.9 %copy-start.6 = (bf16[15,6,90]{2,1,0:T(8,128)(2,1)}, bf16[15,6,90]{2,1,0:T(8,128)(2,1)S(1)}, u32[]{:S(2)}) copy-start(bf16[15,6,90]{2,1,0:T(8,128)(2,1)S(1)} %reshape.223) | copy-start | bytes 48604
  2.5 11.8 %copy-start.4 = (bf16[15,6,1440]{2,1,0:T(8,128)(2,1)}, bf16[15,6,1440]{2,1,0:T(8,128)(2,1)S(1)}, u32[]{:S(2)}) copy-start(bf16[15,6,1440]{2,1,0:T(8,128)(2,1)S(1)} %reshape.222) | copy-start | bytes 777604
  3.4 22.1 %all-to-all-start = ((bf16[16,8,1536]{2,1,0:T(8,128)(2,1)}), bf16[16,8,1536]{2,1,0:T(8,128)(2,1)S(1)}, u32[]{:S(2)}, u32[]{:S(2)}) async-start(bf16[16,8,1536]{2,1,0:T(8,128)(2,1)} %fusion.7), calls=%async_computation | async-start | bytes 786432 | tf_op jit(solution)/shard_map/all_to_all | solution.py:429
  14.3 4.2 %copy-start.8 = (f32[3]{0:T(128)S(1)}, f32[3]{0:T(128)}, u32[]{:S(2)}) copy-start(f32[3]{0:T(128)} %add_convert_fusion.1) | copy-start | bytes 40
  14.3 4.3 %copy-start.9 = (f32[3]{0:T(128)S(1)}, f32[3]{0:T(128)}, u32[]{:S(2)}) copy-start(f32[3]{0:T(128)} %fusion.21) | copy-start | bytes 40
  14.3 5.6 %copy-start.5 = (bf16[15,6,1440]{2,1,0:T(8,128)(2,1)S(1)}, bf16[15,6,1440]{2,1,0:T(8,128)(2,1)}, u32[]{:S(2)}) copy-start(bf16[15,6,1440]{2,1,0:T(8,128)(2,1)} %copy-done.4) | copy-start | bytes 777604
  14.3 5.6 %copy-start.7 = (bf16[15,6,90]{2,1,0:T(8,128)(2,1)S(1)}, bf16[15,6,90]{2,1,0:T(8,128)(2,1)}, u32[]{:S(2)}) copy-start(bf16[15,6,90]{2,1,0:T(8,128)(2,1)} %copy-done.6) | copy-start | bytes 48604
  19.9 19.5 %copy-start.10 = (f32[3]{0:T(128)S(1)}, f32[3]{0:T(128)}, u32[]{:S(2)}) copy-start(f32[3]{0:T(128)} %get-tuple-element.15) | copy-start | bytes 40
  25.6 1.0 copy-start
  27.6 0.7 copy-start.1
  28.3 22.0 %all-to-all-start.1 = ((bf16[128,8,128]{2,1,0:T(8,128)(2,1)}), bf16[128,8,128]{2,1,0:T(8,128)(2,1)}, u32[]{:S(2)}, u32[]{:S(2)}) async-start(bf16[128,8,128]{2,1,0:T(8,128)(2,1)} %bitcast.19), calls=%async_computation.1 | async-start | bytes 524288 | tf_op jit(solution)/shard_map/all_to_all | solution.py:438
  42.4 0.7 copy-start.3
  50.3 18.9 %all-to-all-start.3 = ((bf16[16,8,1536]{2,1,0:T(8,128)(2,1)}), bf16[16,8,1536]{2,1,0:T(8,128)(2,1)S(1)}, u32[]{:S(2)}, u32[]{:S(2)}) async-start(bf16[16,8,1536]{2,1,0:T(8,128)(2,1)} %bitcast.21), calls=%async_computation.3 | async-start | bytes 786432 | tf_op jit(solution)/shard_map/all_to_all | solution.py:447
  68.5 0.7 copy-start.2
  69.2 21.5 %all-to-all-start.2 = ((bf16[128,8,128]{2,1,0:T(8,128)(2,1)}), bf16[128,8,128]{2,1,0:T(8,128)(2,1)}, u32[]{:S(2)}, u32[]{:S(2)}) async-start(bf16[128,8,128]{2,1,0:T(8,128)(2,1)} %bitcast.20), calls=%async_computation.2 | async-start | bytes 524288 | tf_op jit(solution)/shard_map/all_to_all | solution.py:452
  95.9 6.0 %collective-permute-start = (f32[]{:T(128)}, f32[]{:T(128)}, u32[]{:S(2)}, u32[]{:S(2)}) collective-permute-start(f32[]{:T(128)} %fusion.9), channel_id=1, source_target_pairs={{0,128},{128,0},{1,129},{129,1},{2,130},{130,2},{3,131},{131,3},{4... | collective-permute-start | bytes 20 | tf_op jit(solution)/shard_map/ppermute | solution.py:456

commit v2 on v1

v2 whole, which is shorter than its diff:
```python
import functools
import math

import jax
import jax.numpy as jnp
from jax import lax
from jax.experimental import pallas as pl
from jax.experimental.pallas import tpu as pltpu
from jax.sharding import PartitionSpec as P

PARALLEL_LINES = 720
AZIMUTH_STEPS = 1440
DEGREE_CUTOFF = 384
SOFTENING_EPS = 0.25
SPECTRAL_WEIGHT = 0.1

MEMBERS = 16
BANDS = 8
GROUPS = MEMBERS * BANDS
ORDERS = DEGREE_CUTOFF // GROUPS
BAND_ROWS = PARALLEL_LINES // BANDS
LON_BLOCK = AZIMUTH_STEPS // MEMBERS
ROW_GROUPS = 15
GROUP_ROWS = 6
LANES = 128
LON_CHUNKS = 12
LON_PADDED = LON_CHUNKS * LANES
SPECTRAL_ROWS = GROUPS * 8
BLOCK = 16

VMEM = pltpu.VMEM
MESH = pl.DeviceIdType.MESH
F32 = jnp.float32
BF16 = jnp.bfloat16


def params(**kw):
    return pltpu.CompilerParams(vmem_limit_bytes=48 << 20, **kw)


def iota(shape, dim):
    return lax.broadcasted_iota(jnp.int32, shape, dim)


def cos_sin(steps):
    quarter = jnp.floor(steps * (1.0 / 360.0) + 0.5)
    rest = (steps - 360.0 * quarter) * (2.0 * math.pi / AZIMUTH_STEPS)
    quadrant = quarter - 4.0 * jnp.floor(quarter * 0.25)
    square = rest * rest
    sine = rest * (
        1.0
        + square
        * (-1.0 / 6.0 + square * (1.0 / 120.0 + square * (-1.0 / 5040.0 + square * (1.0 / 362880.0))))
    )
    cosine = 1.0 + square * (
        -0.5
        + square
        * (1.0 / 24.0 + square * (-1.0 / 720.0 + square * (1.0 / 40320.0 - square * (1.0 / 3628800.0))))
    )
    odd = (quadrant == 1.0) | (quadrant == 3.0)
    cos_part = jnp.where(odd, sine, cosine)
    sin_part = jnp.where(odd, cosine, sine)
    cos_part = jnp.where((quadrant == 1.0) | (quadrant == 2.0), -cos_part, cos_part)
    sin_part = jnp.where(quadrant >= 2.0, -sin_part, sin_part)
    return cos_part, sin_part


def fill_dft(out_ref):
    def body(block, carry):
        row = block * BLOCK + iota((BLOCK, LANES), 0)
        lane = iota((BLOCK, LANES), 1)
        part = row & 7
        order = (ORDERS * (row >> 3) + (part >> 1)).astype(F32)
        turn = (360 * (part & 1)).astype(F32)
        cosine, sine = cos_sin(order * lane.astype(F32) + turn)
        cosine = jnp.where(part < 2 * ORDERS, cosine, 0.0)
        sine = jnp.where(part < 2 * ORDERS, sine, 0.0)
        cos_step, sin_step = cos_sin(order * float(LANES))
        rows = pl.ds(pl.multiple_of(block * BLOCK, BLOCK), BLOCK)
        for chunk in range(LON_CHUNKS):
            value = cosine
            if chunk == LON_CHUNKS - 1:
                value = jnp.where(lane < AZIMUTH_STEPS - LANES * chunk, value, 0.0)
            out_ref[rows, LANES * chunk : LANES * (chunk + 1)] = value.astype(BF16)
            cosine, sine = (
                cosine * cos_step - sine * sin_step,
                sine * cos_step + cosine * sin_step,
            )
        return carry

    lax.fori_loop(0, SPECTRAL_ROWS // BLOCK, body, 0)


def fill_recurrence(first, out_ref):
    order = (first + iota((8, DEGREE_CUTOFF), 0)).astype(F32)
    degree = iota((8, DEGREE_CUTOFF), 1).astype(F32)
    growing = degree > order
    denominator = jnp.where(growing, degree * degree - order * order, 1.0)
    leading = jnp.sqrt(jnp.maximum(4.0 * degree * degree - 1.0, 0.0) / denominator)
    trailing = jnp.sqrt(
        jnp.maximum(
            ((degree - 1.0) * (degree - 1.0) - order * order)
            * (2.0 * degree + 1.0)
            / ((2.0 * degree - 3.0) * denominator),
            0.0,
        )
    )
    out_ref[0:8, :] = jnp.where(growing, leading, 0.0)
    out_ref[8:16, :] = jnp.where(growing, trailing, 0.0)


def seed_logs(first):
    order = (first + iota((8, DEGREE_CUTOFF), 0)).astype(F32)
    factor = (1 + iota((8, DEGREE_CUTOFF), 1)).astype(F32)
    summands = jnp.where(factor <= order, jnp.log(1.0 - 0.5 / factor), 0.0)
    return 0.5 * jnp.log(order[:, 0:1] + 0.5) + 0.5 * jnp.sum(summands, axis=1, keepdims=True)


def fill_legendre(first, coef_ref, table_ref, out_ref):
    band, lane = iota((8, LANES), 0), iota((8, LANES), 1)
    group, part = lane >> 3, lane & 7
    valid = (group < ROW_GROUPS) & (part < GROUP_ROWS)
    row = jnp.where(valid, BAND_ROWS * band + GROUP_ROWS * group + part, 0)
    cos_lat, sin_lat = cos_sin(row.astype(F32) + 0.5)
    weight = jnp.where(valid, math.pi / PARALLEL_LINES * sin_lat, 0.0)
    log_sin = jnp.log(sin_lat)
    seeds = seed_logs(first)

    def body(block, carry):
        state = list(carry)
        for step in range(BLOCK):
            degree = block * BLOCK + step
            for index in range(ORDERS):
                latest, before, log_scale, factor = state[4 * index : 4 * index + 4]
                leading = coef_ref[index, degree]
                trailing = coef_ref[8 + index, degree]
                begin = jnp.where(degree == first + index, 1.0, 0.0)
                advanced = (leading * cos_lat) * latest + (begin - trailing * before)
                row = (index * DEGREE_CUTOFF + degree) * 8
                table_ref[pl.ds(pl.multiple_of(row, 8), 8), :] = advanced * factor
                state[4 * index : 4 * index + 4] = [advanced, latest, log_scale, factor]
        for index in range(ORDERS):
            latest, before, log_scale, factor = state[4 * index : 4 * index + 4]
            largest = jnp.maximum(jnp.abs(latest), jnp.abs(before))
            largest = jnp.where(largest > 0.0, largest, 1.0)
            shrink = 1.0 / largest
            log_scale = log_scale + jnp.log(largest)
            state[4 * index : 4 * index + 4] = [
                latest * shrink,
                before * shrink,
                log_scale,
                jnp.exp(log_scale) * weight,
            ]
        return tuple(state)

    state = []
    for index in range(ORDERS):
        order = jnp.broadcast_to((first + index).astype(F32), (8, LANES))
        start = jnp.broadcast_to(seeds[index : index + 1, :], (8, LANES)) + order * log_sin
        state += [jnp.zeros((8, LANES), F32), jnp.zeros((8, LANES), F32), start, jnp.exp(start) * weight]
    lax.fori_loop(0, DEGREE_CUTOFF // BLOCK, body, tuple(state))
    for index in range(ORDERS):
        for band in range(BANDS):
            rows = table_ref[pl.ds(index * DEGREE_CUTOFF * 8 + band, DEGREE_CUTOFF, stride=8), :]
            out_ref[index, :, LANES * band : LANES * (band + 1)] = rows.astype(BF16)


def fill_truth(blocks_ref, out_ref):
    lane = iota((8, LANES), 1)
    chunks = [jnp.zeros((8, LANES), F32) for _ in range(LON_CHUNKS)]
    for block in range(MEMBERS):
        first = LON_BLOCK * block
        value = blocks_ref[block].astype(F32)
        shift = first % LANES
        if shift:
            value = pltpu.roll(value, shift, 1)
        for chunk in range(first // LANES, (first + LON_BLOCK - 1) // LANES + 1):
            place = lane + chunk * LANES
            inside = (place >= first) & (place < first + LON_BLOCK)
            chunks[chunk] = jnp.where(inside, value, chunks[chunk])
    for chunk in range(LON_CHUNKS):
        out_ref[:, LANES * chunk : LANES * (chunk + 1)] = chunks[chunk]


def grid_stage(ens, lat, draws_ref, truth_ref, counts_ref):
    row, lane = iota((8, LANES), 0), iota((8, LANES), 1)
    line = (BAND_ROWS * lat + GROUP_ROWS * ens + row).astype(F32)
    weight = jnp.where((row < GROUP_ROWS) & (ens < ROW_GROUPS), cos_sin(line + 0.5)[1], 0.0)

    def body(chunk, total):
        lanes = pl.ds(pl.multiple_of(chunk * LANES, LANES), LANES)
        draws = [draws_ref[i, :, lanes].astype(F32) for i in range(MEMBERS)]
        target = truth_ref[:, lanes]
        counts = [None] * MEMBERS
        for i in range(MEMBERS):
            for k in range(i + 1, MEMBERS):
                above = jnp.where(draws[i] > draws[k], 1.0, 0.0)
                turn = jnp.where(draws[i] < draws[k], -1.0, above)
                counts[i] = turn if counts[i] is None else counts[i] + turn
                counts[k] = -turn if counts[k] is None else counts[k] - turn
        spread = jnp.zeros((8, LANES), F32)
        for i in range(MEMBERS):
            gap = draws[i] - target
            above = jnp.where(draws[i] > target, float(MEMBERS - 1), 0.0)
            side = jnp.where(draws[i] < target, -float(MEMBERS - 1), above)
            counts_ref[i, :, lanes] = (side - counts[i]).astype(BF16)
            spread = spread + (jnp.abs(gap) - (draws[i] * counts[i]) * (1.0 / (MEMBERS - 1)))
        return total + jnp.where(lane + chunk * LANES < AZIMUTH_STEPS, spread, 0.0)

    return weight * lax.fori_loop(0, LON_CHUNKS, body, jnp.zeros((8, LANES), F32))


def spectral_stage(first, grid_loss, modes_ref, table_ref, out_ref, wide_ref, lhs_ref):
    draws = MEMBERS
    scale = SPECTRAL_WEIGHT * PARALLEL_LINES * AZIMUTH_STEPS / (DEGREE_CUTOFF * (DEGREE_CUTOFF + 1) / 2)
    lane = iota((64, LANES), 1)
    target = jnp.zeros((64, LANES), F32)
    for member in range(draws):
        value = modes_ref[8 * member : 8 * member + 8].astype(F32).reshape(64, LANES)
        wide_ref[64 * member : 64 * member + 64, :] = value
        if member < ROW_GROUPS:
            moved = pltpu.roll(value, (8 * member + 8) % LANES, 1)
            target = jnp.where((lane >> 3) == member, moved, target)
    loss = jnp.zeros((1, DEGREE_CUTOFF), F32)
    degree = iota((1, DEGREE_CUTOFF), 1)
    pad = jnp.zeros((14, LANES), F32)
    for index in range(ORDERS):
        for band in range(BANDS):
            lanes = slice(LANES * band, LANES * (band + 1))
            parts = [
                wide_ref[pl.ds(8 * band + 2 * index + r, draws, stride=64), :] for r in range(2)
            ]
            aims = [target[8 * band + 2 * index + r : 8 * band + 2 * index + r + 1, :] for r in range(2)]
            lhs_ref[index, :, lanes] = jnp.concatenate(parts + aims + [pad], axis=0).astype(BF16)
        terms = lax.dot_general(
            lhs_ref[index],
            table_ref[index],
            (((1,), (1,)), ((), ())),
            preferred_element_type=F32,
        )
        real, imag = terms[0:draws], terms[draws : 2 * draws]
        real_aim, imag_aim = terms[2 * draws : 2 * draws + 1], terms[2 * draws + 1 : 2 * draws + 2]
        gap_real, gap_imag = real - real_aim, imag - imag_aim
        square = gap_real * gap_real + gap_imag * gap_imag + SOFTENING_EPS**2
        inverse = lax.rsqrt(square)
        near = square * inverse
        step_real, step_imag = gap_real * inverse, gap_imag * inverse
        pair = jnp.zeros_like(real)
        pull_real, pull_imag = jnp.zeros_like(real), jnp.zeros_like(real)
        for other in range(draws):
            gap_real, gap_imag = real - real[other : other + 1], imag - imag[other : other + 1]
            square = gap_real * gap_real + gap_imag * gap_imag + SOFTENING_EPS**2
            inverse = lax.rsqrt(square)
            pair = pair + square * inverse
            pull_real = pull_real + gap_real * inverse
            pull_imag = pull_imag + gap_imag * inverse
        kept = degree >= first + index
        score = jnp.sum(near, axis=0, keepdims=True) - (
            jnp.sum(pair, axis=0, keepdims=True) - draws * SOFTENING_EPS
        ) / (2.0 * (draws - 1))
        loss = loss + jnp.where(kept, score, 0.0)
        down = jnp.concatenate(
            [step_real - pull_real / (draws - 1), step_imag - pull_imag / (draws - 1)], axis=0
        )
        grad = jnp.where(kept, scale * down, 0.0).astype(BF16)
        back = jnp.dot(grad, table_ref[index], preferred_element_type=F32)
        for band in range(BANDS):
            for r in range(2):
                wide_ref[pl.ds(8 * band + 2 * index + r, draws, stride=64), :] = back[
                    draws * r : draws * (r + 1), LANES * band : LANES * (band + 1)
                ]
    local = jnp.sum(jnp.sum(grid_loss, axis=0, keepdims=True), axis=1, keepdims=True) / (
        PARALLEL_LINES * AZIMUTH_STEPS
    ) + SPECTRAL_WEIGHT / (DEGREE_CUTOFF * (DEGREE_CUTOFF + 1) / 2) * jnp.sum(loss, axis=1, keepdims=True)
    high = local.astype(BF16).astype(F32)
    middle = (local - high).astype(BF16).astype(F32)
    low = local - high - middle
    row = iota((BLOCK, LANES), 0) & 7
    column = iota((BLOCK, LANES), 1)
    spare = jnp.where(column == LANES - 8, high, jnp.where(column == LANES - 7, middle, low))
    carries = (row == 0) & (column >= LANES - 8) & (column < LANES - 5)
    for block in range(SPECTRAL_ROWS // BLOCK):
        value = wide_ref[BLOCK * block : BLOCK * (block + 1), :]
        value = jnp.where(row < 2 * ORDERS, value, 0.0)
        value = jnp.where(carries, spare, value)
        out_ref[2 * block : 2 * block + 2] = value.reshape(2, 8, LANES).astype(BF16)


def exchange_kernel(
    own_ref,
    truth_in_ref,
    dft_ref,
    back_in_ref,
    counts_in_ref,
    loss_ref,
    wide_own_ref,
    rows_out_ref,
    rows_in_ref,
    blocks_out_ref,
    blocks_in_ref,
    truth_ref,
    field_ref,
    modes_out_ref,
    modes_in_ref,
    coef_vector_ref,
    coef_ref,
    table_ref,
    legendre_ref,
    counts_out_ref,
    back_out_ref,
    wide_ref,
    lhs_ref,
    send_sem,
    recv_sem,
    local_sem,
):
    chan, ens, lat = lax.axis_index("chan"), lax.axis_index("ens"), lax.axis_index("lat")
    mine = ens * BANDS + lat
    first = ORDERS * mine

    barrier = pltpu.get_barrier_semaphore()

    def greet(step, carry):
        peer = lax.rem(mine + step, GROUPS)
        pl.semaphore_signal(
            barrier,
            inc=1,
            device_id=(chan, lax.div(peer, BANDS), lax.rem(peer, BANDS)),
            device_id_type=MESH,
        )
        return carry

    lax.fori_loop(1, GROUPS, greet, 0)

    def copy(source, target, kind, peer_ens, peer_lat):
        return pltpu.make_async_remote_copy(
            src_ref=source,
            dst_ref=target,
            send_sem=send_sem.at[kind],
            recv_sem=recv_sem.at[kind],
            device_id=(chan, peer_ens, peer_lat),
            device_id_type=MESH,
        )

    def to_members(source, target, kind):
        def body(step, carry):
            peer = lax.rem(ens + step, MEMBERS)
            copy(source.at[peer], target.at[ens], kind, peer, lat).start()
            return carry

        lax.fori_loop(1, MEMBERS, body, 0)
        target[ens] = source[ens]

    def to_groups(source, target, kind, block):
        def body(step, carry):
            peer = block * 32 + lax.rem(mine + step, 32)

            @pl.when(peer != mine)
            def _():
                copy(source.at[peer], target.at[mine], kind, lax.div(peer, BANDS), lax.rem(peer, BANDS)).start()

            return carry

        lax.fori_loop(0, 32, body, 0)

    def all_of(source, target, kind, count):
        return copy(source.at[pl.ds(0, count)], target.at[pl.ds(0, count)], kind, ens, lat)

    wide_own_ref[88:96, :] = jnp.zeros((8, LON_PADDED), F32)
    wide_own_ref[:, LON_PADDED - LANES :] = jnp.zeros((96, LANES), F32)
    wide_own_ref[0:BAND_ROWS, 0:LON_BLOCK] = truth_in_ref[...].astype(F32)
    for group in range(ROW_GROUPS):
        blocks_out_ref[group] = wide_own_ref[GROUP_ROWS * group : GROUP_ROWS * group + 8, 0:LANES].astype(BF16)
    blocks_out_ref[ROW_GROUPS] = jnp.zeros((8, LANES), BF16)
    wide_own_ref[0:BAND_ROWS, 0:AZIMUTH_STEPS] = own_ref[...].astype(F32)
    for group in range(ROW_GROUPS):
        rows_out_ref[group] = wide_own_ref[GROUP_ROWS * group : GROUP_ROWS * group + 8, :].astype(BF16)
    rows_out_ref[ROW_GROUPS] = jnp.zeros((8, LON_PADDED), BF16)

    pl.semaphore_wait(barrier, GROUPS - 1)
    to_members(blocks_out_ref, blocks_in_ref, 0)
    to_members(rows_out_ref, rows_in_ref, 1)

    fill_recurrence(first, coef_vector_ref)
    coef_copy = pltpu.make_async_copy(coef_vector_ref, coef_ref, local_sem)
    coef_copy.start()
    for pair in range(7):
        both = [
            wide_own_ref[GROUP_ROWS * group : GROUP_ROWS * group + 8, :] for group in (2 * pair, 2 * pair + 1)
        ]
        field_ref[16 * pair : 16 * pair + 16, :] = jnp.concatenate(both, axis=0).astype(BF16)
    fill_dft(dft_ref)

    all_of(blocks_out_ref, blocks_in_ref, 0, MEMBERS - 1).wait_recv()
    fill_truth(blocks_in_ref, truth_ref)
    both = [wide_own_ref[84:92, :], truth_ref[...]]
    field_ref[112:128, :] = jnp.concatenate(both, axis=0).astype(BF16)

    def fourier(step, carry):
        block = lax.rem(lax.div(mine, 32) + step, 4)
        modes = lax.dot_general(
            dft_ref[pl.ds(pl.multiple_of(block * 256, 256), 256), :],
            field_ref[...],
            (((1,), (1,)), ((), ())),
            preferred_element_type=F32,
        )
        modes_out_ref[pl.ds(block * 32, 32)] = modes.reshape(32, 8, LANES).astype(BF16)
        to_groups(modes_out_ref, modes_in_ref, 2, block)
        return carry

    lax.fori_loop(0, 4, fourier, 0)
    modes_in_ref[mine] = modes_out_ref[mine]

    coef_copy.wait()
    fill_legendre(first, coef_ref, table_ref, legendre_ref)

    all_of(rows_out_ref, rows_in_ref, 1, MEMBERS - 1).wait_recv()
    grid_loss = grid_stage(ens, lat, rows_in_ref, truth_ref, counts_out_ref)
    to_members(counts_out_ref, counts_in_ref, 3)

    all_of(modes_out_ref, modes_in_ref, 2, GROUPS - 1).wait_recv()
    spectral_stage(first, grid_loss, modes_in_ref, legendre_ref, back_out_ref, wide_ref, lhs_ref)

    def give_back(step, carry):
        to_groups(back_out_ref, back_in_ref, 4, lax.rem(lax.div(mine, 32) + step, 4))
        return carry

    lax.fori_loop(0, 4, give_back, 0)
    back_in_ref[mine] = back_out_ref[mine]

    all_of(counts_out_ref, counts_in_ref, 3, MEMBERS - 1).wait_recv()
    all_of(back_out_ref, back_in_ref, 4, GROUPS - 1).wait_recv()
    total = jnp.zeros((8, LANES), F32)
    for block in range(16):
        total = total + jnp.sum(back_in_ref[8 * block : 8 * block + 8].astype(F32), axis=0)
    row, column = iota((8, LANES), 0), iota((8, LANES), 1)
    total = jnp.where((row == 0) & (column >= LANES - 8) & (column < LANES - 5), total, 0.0)
    loss_ref[...] = jnp.sum(jnp.sum(total, axis=0, keepdims=True), axis=1, keepdims=True)

    all_of(blocks_out_ref, blocks_in_ref, 0, MEMBERS - 1).wait_send()
    all_of(rows_out_ref, rows_in_ref, 1, MEMBERS - 1).wait_send()
    all_of(modes_out_ref, modes_in_ref, 2, GROUPS - 1).wait_send()
    all_of(counts_out_ref, counts_in_ref, 3, MEMBERS - 1).wait_send()
    all_of(back_out_ref, back_in_ref, 4, GROUPS - 1).wait_send()


def exchange(own, target):
    rows = (MEMBERS, 8, LON_PADDED)
    blocks = (MEMBERS, 8, LANES)
    modes = (GROUPS, 8, LANES)
    return pl.pallas_call(
        exchange_kernel,
        out_shape=(
            jax.ShapeDtypeStruct((SPECTRAL_ROWS, LON_PADDED), BF16),
            jax.ShapeDtypeStruct(modes, BF16),
            jax.ShapeDtypeStruct(rows, BF16),
            jax.ShapeDtypeStruct((1, 1), F32),
        ),
        in_specs=[pl.BlockSpec(memory_space=VMEM)] * 2,
        out_specs=tuple([pl.BlockSpec(memory_space=VMEM)] * 4),
        scratch_shapes=[
            VMEM((96, LON_PADDED), F32),
            VMEM(rows, BF16),
            VMEM(rows, BF16),
            VMEM(blocks, BF16),
            VMEM(blocks, BF16),
            VMEM((8, LON_PADDED), F32),
            VMEM((LANES, LON_PADDED), BF16),
            VMEM(modes, BF16),
            VMEM(modes, BF16),
            VMEM((16, DEGREE_CUTOFF), F32),
            pltpu.SMEM((16, DEGREE_CUTOFF), F32),
            VMEM((ORDERS * DEGREE_CUTOFF * 8, LANES), F32),
            VMEM((ORDERS, DEGREE_CUTOFF, BANDS * LANES), BF16),
            VMEM(rows, BF16),
            VMEM(modes, BF16),
            VMEM((SPECTRAL_ROWS, LANES), F32),
            VMEM((ORDERS, 48, BANDS * LANES), BF16),
            pltpu.SemaphoreType.DMA((5,)),
            pltpu.SemaphoreType.DMA((5,)),
            pltpu.SemaphoreType.DMA,
        ],
        compiler_params=params(collective_id=0, has_side_effects=True),
        cost_estimate=pl.CostEstimate(flops=800_000_000, bytes_accessed=8 << 20, transcendentals=0),
    )(own, target)


def final_kernel(table_ref, modes_ref, counts_ref, out_ref):
    row = iota((LANES, LANES), 0)
    line = BAND_ROWS * lax.axis_index("lat") + GROUP_ROWS * (row >> 3) + (row & 7)
    weight = cos_sin(line.astype(F32) + 0.5)[1] / (MEMBERS - 1)
    for chunk in range(LON_CHUNKS):
        lanes = slice(LANES * chunk, LANES * (chunk + 1))
        width = min(LANES, AZIMUTH_STEPS - LANES * chunk)
        wave = lax.dot_general(
            modes_ref[...],
            table_ref[:, lanes],
            (((0,), (0,)), ((), ())),
            preferred_element_type=F32,
        )
        total = weight * counts_ref[:, lanes].astype(F32) + wave
        for group in range(ROW_GROUPS):
            out_ref[
                GROUP_ROWS * group : GROUP_ROWS * (group + 1), 0, LANES * chunk : LANES * chunk + width
            ] = total[8 * group : 8 * group + GROUP_ROWS, 0:width]


def final(table, modes, counts):
    return pl.pallas_call(
        final_kernel,
        out_shape=jax.ShapeDtypeStruct((BAND_ROWS, 1, AZIMUTH_STEPS), F32),
        in_specs=[pl.BlockSpec(memory_space=VMEM)] * 3,
        out_specs=pl.BlockSpec(memory_space=VMEM),
        compiler_params=params(),
        cost_estimate=pl.CostEstimate(flops=400_000_000, bytes_accessed=4 << 20, transcendentals=0),
    )(table, modes, counts)


def local(model_outputs, verifying_truth):
    table, back, counts, shared = exchange(model_outputs[0, 0], verifying_truth[0])
    other = lax.ppermute(shared, "chan", [(0, 1), (1, 0)])
    slope = final(table, back.reshape(SPECTRAL_ROWS, LANES), counts.reshape(LANES, LON_PADDED))
    return (slope.reshape(1, 1, BAND_ROWS, AZIMUTH_STEPS), (shared + other)[0, 0])


def solution(mesh):
    return jax.shard_map(
        local,
        mesh=mesh,
        in_specs=(P("ens", "chan", "lat", None), P("chan", "lat", "ens")),
        out_specs=(P("ens", "chan", "lat", None), P()),
        check_vma=False,
    )
```

time: 105 us -> 55 us (0.52)
  starting transfers between devices: 39.6 us -> 3.03 us
  Pallas kernels: 17.7 us -> 47.1 us
  waiting for transfers between devices: 23.8 us -> 0.01 us
  other arithmetic: 10.7 us -> 0 us
  local copies, waits for them, and re-layouts: 9.21 us -> 1.69 us
    all_to_all x4 -> x0, starting transfers between devices: 34.5 us -> none  [the longest x1 11 us: local(): lax.all_to_all(modes.reshape(GROUPS, 8, LANES), ('ens', 'lat'), split_axi...]
    pallas_call x6 -> x2, Pallas kernels: 17.7 us -> 47.1 us  [the longest x1 45.1 us: exchange(): pl.pallas_call(exchange_kernel, out_shape=(jax.ShapeDtypeStruct((SPECTRAL...]
    all_to_all x4 -> x0, waiting for transfers between devices: 22.9 us -> none  [the longest x1 10.9 us: local(): lax.all_to_all(back.reshape(GROUPS, 8, LANES), ('ens', 'lat'), split_axis...]
    unnamed x23 -> x4, local copies, waits for them, and re-layouts: 4.53 us -> 1.69 us
    ppermute x1, starting transfers between devices: 5.09 us -> 3.03 us  [local(): other = lax.ppermute(shared, 'chan', [(0, 1), (1, 0)])]
    reshape x2 -> x0, local copies, waits for them, and re-layouts: 1.86 us -> none  [the longest x1 1.1 us: local(): own = model_outputs.reshape(ROW_GROUPS, GROUP_ROWS, AZIMUTH_STEPS)]
    reduce_sum x1 -> x0, other arithmetic: 1.76 us -> none  [local(): shared = jnp.sum(back[:, 0, LANES - 8:LANES - 5].astype(F32))]
    concatenate x2 -> x0, other arithmetic: 1.64 us -> none  [the longest x1 0.92 us: local(): outgoing = jnp.concatenate([own, target], axis=2)]
  transfers between devices with their start and end apart: 5 -> 1, of which waited for: 4 -> 0; matrix products, arithmetic and copies ran while one was open for 10% -> 0% of each run, Pallas kernels for 14% -> 4%
where the time goes in v2:
time: 55 us; the launch traced here: 54.8 us
  Pallas kernels  47.1 us (86%)
  starting transfers between devices  3.03 us (6%)
  between operations  3 us (5%)
  local copies, waits for them, and re-layouts  1.69 us (3%)
    pallas_call x1, Pallas kernels, exchange(): pl.pallas_call(exchange_kernel, out_shape=(jax.ShapeDtypeStruct((SPECTRAL...  45.1 us
    ppermute x1, starting transfers between devices, local(): other = lax.ppermute(shared, 'chan', [(0, 1), (1, 0)])  3.03 us
    pallas_call x1, Pallas kernels, final(): pl.pallas_call(final_kernel, out_shape=jax.ShapeDtypeStruct((BAND_ROWS, 1...  2.06 us
    unnamed x4, local copies, waits for them, and re-layouts  1.69 us
  transfers between devices with their start and end apart: 1, of which 0 were waited for; matrix products, arithmetic and copies ran while one was open for 0% of the time, Pallas kernels for 4%

profile of v2, /device:TPU:1, one launch (start us, length us, event | category | flops | bytes accessed | tf_op | source)
XLA Modules:
  0.0 54.8 jit_solution(14049697969086073343)
XLA Ops:
  0.6 0.0 copy-start
  0.6 1.0 %copy-done = bf16[1,1,90,1440]{3,2,1,0:T(8,128)(2,1)S(1)} copy-done((bf16[1,1,90,1440]{3,2,1,0:T(8,128)(2,1)S(1)}, bf16[1,1,90,1440]{3,2,1,0:T(8,128)(2,1)}, u32[]{:S(2)}) %copy-start) | copy-done | bytes 259224
  1.6 0.0 copy-start.1
  1.6 0.7 %copy-done.1 = bf16[1,90,90]{2,1,0:T(8,128)(2,1)S(1)} copy-done((bf16[1,90,90]{2,1,0:T(8,128)(2,1)S(1)}, bf16[1,90,90]{2,1,0:T(8,128)(2,1)}, u32[]{:S(2)}) %copy-start.1) | copy-done | bytes 16224
  2.3 45.1 %shard_map.41 = (bf16[1024,1536]{1,0:T(8,128)(2,1)S(1)}, bf16[128,8,128]{2,1,0:T(8,128)(2,1)S(1)}, bf16[16,8,1536]{2,1,0:T(8,128)(2,1)S(1)}, f32[1,1]{1,0:T(1,128)}) custom-call(bf16[90,1440]{1,0:T(8,128)(2,1)S(1)} %bitcast.10, bf16[90,90]{1,0:T(8,128)(2,1)S(1)} %bitcast.11), custom_call_target="tpu_custom_call" | custom-call | flops 800000000 | bytes 8388608 | tf_op jit(solution)/shard_map/pallas_call | solution.py:451
  47.4 3.0 %collective-permute-start = (f32[1,1]{1,0:T(1,128)}, f32[1,1]{1,0:T(1,128)}, u32[]{:S(2)}, u32[]{:S(2)}) collective-permute-start(f32[1,1]{1,0:T(1,128)} %get-tuple-element.9), channel_id=1, source_target_pairs={{0,128},{128,0},{1,129},{129,1},{2,130},{130,2},{3,131},{131,3},{4... | collective-permute-start | bytes 20 | tf_op jit(solution)/shard_map/ppermute | solution.py:521
  50.4 2.1 %shard_map.42 = f32[90,1,1440]{2,1,0:T(1,128)} custom-call(bf16[1024,1536]{1,0:T(8,128)(2,1)S(1)} %get-tuple-element.6.table_ref, bf16[1024,128]{1,0:T(8,128)(2,1)S(1)} %bitcast.9, bf16[128,1536]{1,0:T(8,128)(2,1)S(1)} %bitcast.8), custom_call_target="tpu_custom_call" | custom-call | flops 400000000 | bytes 4194304 | tf_op jit(solution)/shard_map/pallas_call | solution.py:509
  52.5 0.0 collective-permute-done
Async XLA Ops:
  0.6 1.0 %copy-start = (bf16[1,1,90,1440]{3,2,1,0:T(8,128)(2,1)S(1)}, bf16[1,1,90,1440]{3,2,1,0:T(8,128)(2,1)}, u32[]{:S(2)}) copy-start(bf16[1,1,90,1440]{3,2,1,0:T(8,128)(2,1)} %param.2) | copy-start | bytes 777604
  1.6 0.7 %copy-start.1 = (bf16[1,90,90]{2,1,0:T(8,128)(2,1)S(1)}, bf16[1,90,90]{2,1,0:T(8,128)(2,1)}, u32[]{:S(2)}) copy-start(bf16[1,90,90]{2,1,0:T(8,128)(2,1)} %param.3) | copy-start | bytes 48604
  47.4 5.1 %collective-permute-start = (f32[1,1]{1,0:T(1,128)}, f32[1,1]{1,0:T(1,128)}, u32[]{:S(2)}, u32[]{:S(2)}) collective-permute-start(f32[1,1]{1,0:T(1,128)} %get-tuple-element.9), channel_id=1, source_target_pairs={{0,128},{128,0},{1,129},{129,1},{2,130},{130,2},{3,131},{131,3},{4... | collective-permute-start | bytes 20 | tf_op jit(solution)/shard_map/ppermute | solution.py:521

commit v3 on v2

--- a/solution.py
+++ b/solution.py
@@ -25,8 +25,12 @@
 LANES = 128
 LON_CHUNKS = 12
 LON_PADDED = LON_CHUNKS * LANES
-SPECTRAL_ROWS = GROUPS * 8
+SPECTRAL_ROWS = 2 * DEGREE_CUTOFF
 BLOCK = 16
+DFT_BLOCK = 64
+PACKED_ROWS = GROUP_ROWS * LON_CHUNKS
+PACKED_TILES = PACKED_ROWS // 8
+PARTS = 2 * ORDERS
 
 VMEM = pltpu.VMEM
 MESH = pl.DeviceIdType.MESH
@@ -67,16 +71,13 @@
 
 def fill_dft(out_ref):
     def body(block, carry):
-        row = block * BLOCK + iota((BLOCK, LANES), 0)
-        lane = iota((BLOCK, LANES), 1)
-        part = row & 7
-        order = (ORDERS * (row >> 3) + (part >> 1)).astype(F32)
-        turn = (360 * (part & 1)).astype(F32)
+        row = block * DFT_BLOCK + iota((DFT_BLOCK, LANES), 0)
+        lane = iota((DFT_BLOCK, LANES), 1)
+        order = (row >> 1).astype(F32)
+        turn = (360 * (row & 1)).astype(F32)
         cosine, sine = cos_sin(order * lane.astype(F32) + turn)
-        cosine = jnp.where(part < 2 * ORDERS, cosine, 0.0)
-        sine = jnp.where(part < 2 * ORDERS, sine, 0.0)
         cos_step, sin_step = cos_sin(order * float(LANES))
-        rows = pl.ds(pl.multiple_of(block * BLOCK, BLOCK), BLOCK)
+        rows = pl.ds(pl.multiple_of(block * DFT_BLOCK, DFT_BLOCK), DFT_BLOCK)
         for chunk in range(LON_CHUNKS):
             value = cosine
             if chunk == LON_CHUNKS - 1:
@@ -88,7 +89,7 @@
             )
         return carry
 
-    lax.fori_loop(0, SPECTRAL_ROWS // BLOCK, body, 0)
+    lax.fori_loop(0, SPECTRAL_ROWS // DFT_BLOCK, body, 0)
 
 
 def fill_recurrence(first, out_ref):
@@ -165,7 +166,7 @@
             out_ref[index, :, LANES * band : LANES * (band + 1)] = rows.astype(BF16)
 
 
-def fill_truth(blocks_ref, out_ref):
+def fill_truth(blocks_ref, out_ref, packed_ref):
     lane = iota((8, LANES), 1)
     chunks = [jnp.zeros((8, LANES), F32) for _ in range(LON_CHUNKS)]
     for block in range(MEMBERS):
@@ -180,17 +181,21 @@
             chunks[chunk] = jnp.where(inside, value, chunks[chunk])
     for chunk in range(LON_CHUNKS):
         out_ref[:, LANES * chunk : LANES * (chunk + 1)] = chunks[chunk]
+        packed_ref[GROUP_ROWS * chunk : GROUP_ROWS * (chunk + 1), :] = chunks[chunk][0:GROUP_ROWS]
 
 
 def grid_stage(ens, lat, draws_ref, truth_ref, counts_ref):
     row, lane = iota((8, LANES), 0), iota((8, LANES), 1)
-    line = (BAND_ROWS * lat + GROUP_ROWS * ens + row).astype(F32)
-    weight = jnp.where((row < GROUP_ROWS) & (ens < ROW_GROUPS), cos_sin(line + 0.5)[1], 0.0)
-
-    def body(chunk, total):
-        lanes = pl.ds(pl.multiple_of(chunk * LANES, LANES), LANES)
-        draws = [draws_ref[i, :, lanes].astype(F32) for i in range(MEMBERS)]
-        target = truth_ref[:, lanes]
+
+    def body(tile, total):
+        place = 8 * tile + row
+        chunk = (place * 43) >> 8
+        part = place - GROUP_ROWS * chunk
+        line = (BAND_ROWS * lat + GROUP_ROWS * ens + part).astype(F32)
+        kept = (lane + chunk * LANES < AZIMUTH_STEPS) & (ens < ROW_GROUPS)
+        weight = jnp.where(kept, cos_sin(line + 0.5)[1], 0.0)
+        draws = [draws_ref[i, tile].astype(F32) for i in range(MEMBERS)]
+        target = truth_ref[pl.ds(pl.multiple_of(8 * tile, 8), 8), :]
         counts = [None] * MEMBERS
         for i in range(MEMBERS):
             for k in range(i + 1, MEMBERS):
@@ -203,21 +208,22 @@
             gap = draws[i] - target
             above = jnp.where(draws[i] > target, float(MEMBERS - 1), 0.0)
             side = jnp.where(draws[i] < target, -float(MEMBERS - 1), above)
-            counts_ref[i, :, lanes] = (side - counts[i]).astype(BF16)
+            counts_ref[i, tile] = (side - counts[i]).astype(BF16)
             spread = spread + (jnp.abs(gap) - (draws[i] * counts[i]) * (1.0 / (MEMBERS - 1)))
-        return total + jnp.where(lane + chunk * LANES < AZIMUTH_STEPS, spread, 0.0)
-
-    return weight * lax.fori_loop(0, LON_CHUNKS, body, jnp.zeros((8, LANES), F32))
+        return total + jnp.where(kept, weight * spread, 0.0)
+
+    return lax.fori_loop(0, PACKED_TILES, body, jnp.zeros((8, LANES), F32))
 
 
 def spectral_stage(first, grid_loss, modes_ref, table_ref, out_ref, wide_ref, lhs_ref):
     draws = MEMBERS
     scale = SPECTRAL_WEIGHT * PARALLEL_LINES * AZIMUTH_STEPS / (DEGREE_CUTOFF * (DEGREE_CUTOFF + 1) / 2)
-    lane = iota((64, LANES), 1)
-    target = jnp.zeros((64, LANES), F32)
+    held = BANDS * PARTS
+    lane = iota((held, LANES), 1)
+    target = jnp.zeros((held, LANES), F32)
     for member in range(draws):
-        value = modes_ref[8 * member : 8 * member + 8].astype(F32).reshape(64, LANES)
-        wide_ref[64 * member : 64 * member + 64, :] = value
+        value = modes_ref[8 * member : 8 * member + 8].astype(F32).reshape(held, LANES)
+        wide_ref[held * member : held * (member + 1), :] = value
         if member < ROW_GROUPS:
             moved = pltpu.roll(value, (8 * member + 8) % LANES, 1)
             target = jnp.where((lane >> 3) == member, moved, target)
@@ -228,9 +234,10 @@
         for band in range(BANDS):
             lanes = slice(LANES * band, LANES * (band + 1))
             parts = [
-                wide_ref[pl.ds(8 * band + 2 * index + r, draws, stride=64), :] for r in range(2)
+                wide_ref[pl.ds(PARTS * band + 2 * index + r, draws, stride=held), :] for r in range(2)
             ]
-            aims = [target[8 * band + 2 * index + r : 8 * band + 2 * index + r + 1, :] for r in range(2)]
+            aim = PARTS * band + 2 * index
+            aims = [target[aim + r : aim + r + 1, :] for r in range(2)]
             lhs_ref[index, :, lanes] = jnp.concatenate(parts + aims + [pad], axis=0).astype(BF16)
         terms = lax.dot_general(
             lhs_ref[index],
@@ -266,7 +273,7 @@
         back = jnp.dot(grad, table_ref[index], preferred_element_type=F32)
         for band in range(BANDS):
             for r in range(2):
-                wide_ref[pl.ds(8 * band + 2 * index + r, draws, stride=64), :] = back[
+                wide_ref[pl.ds(PARTS * band + 2 * index + r, draws, stride=held), :] = back[
                     draws * r : draws * (r + 1), LANES * band : LANES * (band + 1)
                 ]
     local = jnp.sum(jnp.sum(grid_loss, axis=0, keepdims=True), axis=1, keepdims=True) / (
@@ -275,24 +282,28 @@
     high = local.astype(BF16).astype(F32)
     middle = (local - high).astype(BF16).astype(F32)
     low = local - high - middle
-    row = iota((BLOCK, LANES), 0) & 7
-    column = iota((BLOCK, LANES), 1)
+    row = iota((BANDS, ORDERS, 2, LANES), 1) + iota((BANDS, ORDERS, 2, LANES), 2)
+    column = iota((BANDS, ORDERS, 2, LANES), 3)
+    high, middle, low = (v.reshape(1, 1, 1, 1) for v in (high, middle, low))
     spare = jnp.where(column == LANES - 8, high, jnp.where(column == LANES - 7, middle, low))
     carries = (row == 0) & (column >= LANES - 8) & (column < LANES - 5)
-    for block in range(SPECTRAL_ROWS // BLOCK):
-        value = wide_ref[BLOCK * block : BLOCK * (block + 1), :]
-        value = jnp.where(row < 2 * ORDERS, value, 0.0)
+    for member in range(draws):
+        value = wide_ref[held * member : held * (member + 1), :].reshape(BANDS, ORDERS, 2, LANES)
         value = jnp.where(carries, spare, value)
-        out_ref[2 * block : 2 * block + 2] = value.reshape(2, 8, LANES).astype(BF16)
+        out_ref[BANDS * member : BANDS * (member + 1)] = value.astype(BF16)
 
 
 def exchange_kernel(
-    own_ref,
-    truth_in_ref,
+    own_hbm_ref,
+    truth_hbm_ref,
     dft_ref,
     back_in_ref,
     counts_in_ref,
     loss_ref,
+    own_ref,
+    truth_in_ref,
+    packed_ref,
+    truth_packed_ref,
     wide_own_ref,
     rows_out_ref,
     rows_in_ref,
@@ -317,6 +328,10 @@
     chan, ens, lat = lax.axis_index("chan"), lax.axis_index("ens"), lax.axis_index("lat")
     mine = ens * BANDS + lat
     first = ORDERS * mine
+    truth_copy = pltpu.make_async_copy(truth_hbm_ref, truth_in_ref, local_sem.at[0])
+    truth_copy.start()
+    own_copy = pltpu.make_async_copy(own_hbm_ref, own_ref, local_sem.at[1])
+    own_copy.start()
 
     barrier = pltpu.get_barrier_semaphore()
 
@@ -368,21 +383,27 @@
 
     wide_own_ref[88:96, :] = jnp.zeros((8, LON_PADDED), F32)
     wide_own_ref[:, LON_PADDED - LANES :] = jnp.zeros((96, LANES), F32)
+    truth_copy.wait()
     wide_own_ref[0:BAND_ROWS, 0:LON_BLOCK] = truth_in_ref[...].astype(F32)
     for group in range(ROW_GROUPS):
         blocks_out_ref[group] = wide_own_ref[GROUP_ROWS * group : GROUP_ROWS * group + 8, 0:LANES].astype(BF16)
     blocks_out_ref[ROW_GROUPS] = jnp.zeros((8, LANES), BF16)
+    pl.semaphore_wait(barrier, GROUPS - 1)
+    to_members(blocks_out_ref, blocks_in_ref, 0)
+
+    own_copy.wait()
     wide_own_ref[0:BAND_ROWS, 0:AZIMUTH_STEPS] = own_ref[...].astype(F32)
     for group in range(ROW_GROUPS):
-        rows_out_ref[group] = wide_own_ref[GROUP_ROWS * group : GROUP_ROWS * group + 8, :].astype(BF16)
-    rows_out_ref[ROW_GROUPS] = jnp.zeros((8, LON_PADDED), BF16)
-
-    pl.semaphore_wait(barrier, GROUPS - 1)
-    to_members(blocks_out_ref, blocks_in_ref, 0)
+        for chunk in range(LON_CHUNKS):
+            packed_ref[GROUP_ROWS * chunk : GROUP_ROWS * (chunk + 1), :] = wide_own_ref[
+                GROUP_ROWS * group : GROUP_ROWS * (group + 1), LANES * chunk : LANES * (chunk + 1)
+            ]
+        rows_out_ref[group] = packed_ref[...].reshape(PACKED_TILES, 8, LANES).astype(BF16)
+    rows_out_ref[ROW_GROUPS] = jnp.zeros((PACKED_TILES, 8, LANES), BF16)
     to_members(rows_out_ref, rows_in_ref, 1)
 
     fill_recurrence(first, coef_vector_ref)
-    coef_copy = pltpu.make_async_copy(coef_vector_ref, coef_ref, local_sem)
+    coef_copy = pltpu.make_async_copy(coef_vector_ref, coef_ref, local_sem.at[2])
     coef_copy.start()
     for pair in range(7):
         both = [
@@ -392,19 +413,19 @@
     fill_dft(dft_ref)
 
     all_of(blocks_out_ref, blocks_in_ref, 0, MEMBERS - 1).wait_recv()
-    fill_truth(blocks_in_ref, truth_ref)
+    fill_truth(blocks_in_ref, truth_ref, truth_packed_ref)
     both = [wide_own_ref[84:92, :], truth_ref[...]]
     field_ref[112:128, :] = jnp.concatenate(both, axis=0).astype(BF16)
 
     def fourier(step, carry):
         block = lax.rem(lax.div(mine, 32) + step, 4)
         modes = lax.dot_general(
-            dft_ref[pl.ds(pl.multiple_of(block * 256, 256), 256), :],
+            dft_ref[pl.ds(pl.multiple_of(block * 192, 192), 192), :],
             field_ref[...],
             (((1,), (1,)), ((), ())),
             preferred_element_type=F32,
         )
-        modes_out_ref[pl.ds(block * 32, 32)] = modes.reshape(32, 8, LANES).astype(BF16)
+        modes_out_ref[pl.ds(block * 32, 32)] = modes.reshape(32, ORDERS, 2, LANES).astype(BF16)
         to_groups(modes_out_ref, modes_in_ref, 2, block)
         return carry
 
@@ -415,7 +436,7 @@
     fill_legendre(first, coef_ref, table_ref, legendre_ref)
 
     all_of(rows_out_ref, rows_in_ref, 1, MEMBERS - 1).wait_recv()
-    grid_loss = grid_stage(ens, lat, rows_in_ref, truth_ref, counts_out_ref)
+    grid_loss = grid_stage(ens, lat, rows_in_ref, truth_packed_ref, counts_out_ref)
     to_members(counts_out_ref, counts_in_ref, 3)
 
     all_of(modes_out_ref, modes_in_ref, 2, GROUPS - 1).wait_recv()
@@ -430,10 +451,10 @@
 
     all_of(counts_out_ref, counts_in_ref, 3, MEMBERS - 1).wait_recv()
     all_of(back_out_ref, back_in_ref, 4, GROUPS - 1).wait_recv()
-    total = jnp.zeros((8, LANES), F32)
+    total = jnp.zeros((2, LANES), F32)
     for block in range(16):
-        total = total + jnp.sum(back_in_ref[8 * block : 8 * block + 8].astype(F32), axis=0)
-    row, column = iota((8, LANES), 0), iota((8, LANES), 1)
+        total = total + jnp.sum(back_in_ref[8 * block : 8 * block + 8, 0].astype(F32), axis=0)
+    row, column = iota((2, LANES), 0), iota((2, LANES), 1)
     total = jnp.where((row == 0) & (column >= LANES - 8) & (column < LANES - 5), total, 0.0)
     loss_ref[...] = jnp.sum(jnp.sum(total, axis=0, keepdims=True), axis=1, keepdims=True)
 
@@ -445,9 +466,9 @@
 
 
 def exchange(own, target):
-    rows = (MEMBERS, 8, LON_PADDED)
+    rows = (MEMBERS, PACKED_TILES, 8, LANES)
     blocks = (MEMBERS, 8, LANES)
-    modes = (GROUPS, 8, LANES)
+    modes = (GROUPS, ORDERS, 2, LANES)
     return pl.pallas_call(
         exchange_kernel,
         out_shape=(
@@ -456,9 +477,13 @@
             jax.ShapeDtypeStruct(rows, BF16),
             jax.ShapeDtypeStruct((1, 1), F32),
         ),
-        in_specs=[pl.BlockSpec(memory_space=VMEM)] * 2,
+        in_specs=[pl.BlockSpec(memory_space=pltpu.HBM)] * 2,
         out_specs=tuple([pl.BlockSpec(memory_space=VMEM)] * 4),
         scratch_shapes=[
+            VMEM((BAND_ROWS, AZIMUTH_STEPS), BF16),
+            VMEM((BAND_ROWS, LON_BLOCK), BF16),
+            VMEM((PACKED_ROWS, LANES), F32),
+            VMEM((PACKED_ROWS, LANES), F32),
             VMEM((96, LON_PADDED), F32),
             VMEM(rows, BF16),
             VMEM(rows, BF16),
@@ -478,17 +503,21 @@
             VMEM((ORDERS, 48, BANDS * LANES), BF16),
             pltpu.SemaphoreType.DMA((5,)),
             pltpu.SemaphoreType.DMA((5,)),
-            pltpu.SemaphoreType.DMA,
+            pltpu.SemaphoreType.DMA((3,)),
         ],
         compiler_params=params(collective_id=0, has_side_effects=True),
         cost_estimate=pl.CostEstimate(flops=800_000_000, bytes_accessed=8 << 20, transcendentals=0),
     )(own, target)
 
 
-def final_kernel(table_ref, modes_ref, counts_ref, out_ref):
+def final_kernel(table_ref, modes_ref, counts_ref, out_ref, packed_ref):
     row = iota((LANES, LANES), 0)
     line = BAND_ROWS * lax.axis_index("lat") + GROUP_ROWS * (row >> 3) + (row & 7)
     weight = cos_sin(line.astype(F32) + 0.5)[1] / (MEMBERS - 1)
+    for group in range(ROW_GROUPS):
+        packed_ref[PACKED_ROWS * group : PACKED_ROWS * (group + 1), :] = (
+            counts_ref[group].astype(F32).reshape(PACKED_ROWS, LANES)
+        )
     for chunk in range(LON_CHUNKS):
         lanes = slice(LANES * chunk, LANES * (chunk + 1))
         width = min(LANES, AZIMUTH_STEPS - LANES * chunk)
@@ -498,11 +527,13 @@
             (((0,), (0,)), ((), ())),
             preferred_element_type=F32,
         )
-        total = weight * counts_ref[:, lanes].astype(F32) + wave
         for group in range(ROW_GROUPS):
+            first = PACKED_ROWS * group + GROUP_ROWS * chunk
+            rows = slice(8 * group, 8 * group + GROUP_ROWS)
+            total = weight[rows] * packed_ref[first : first + GROUP_ROWS, :] + wave[rows]
             out_ref[
                 GROUP_ROWS * group : GROUP_ROWS * (group + 1), 0, LANES * chunk : LANES * chunk + width
-            ] = total[8 * group : 8 * group + GROUP_ROWS, 0:width]
+            ] = total[:, 0:width]
 
 
 def final(table, modes, counts):
@@ -511,6 +542,7 @@
         out_shape=jax.ShapeDtypeStruct((BAND_ROWS, 1, AZIMUTH_STEPS), F32),
         in_specs=[pl.BlockSpec(memory_space=VMEM)] * 3,
         out_specs=pl.BlockSpec(memory_space=VMEM),
+        scratch_shapes=[VMEM((ROW_GROUPS * PACKED_ROWS, LANES), F32)],
         compiler_params=params(),
         cost_estimate=pl.CostEstimate(flops=400_000_000, bytes_accessed=4 << 20, transcendentals=0),
     )(table, modes, counts)
@@ -519,7 +551,7 @@
 def local(model_outputs, verifying_truth):
     table, back, counts, shared = exchange(model_outputs[0, 0], verifying_truth[0])
     other = lax.ppermute(shared, "chan", [(0, 1), (1, 0)])
-    slope = final(table, back.reshape(SPECTRAL_ROWS, LANES), counts.reshape(LANES, LON_PADDED))
+    slope = final(table, back.reshape(SPECTRAL_ROWS, LANES), counts)
     return (slope.reshape(1, 1, BAND_ROWS, AZIMUTH_STEPS), (shared + other)[0, 0])
 
 

time: 55 us -> 50.3 us (0.915)
  Pallas kernels: 47.1 us -> 42.6 us
    pallas_call x1, Pallas kernels: 45.1 us -> 40.7 us  [exchange(): pl.pallas_call(exchange_kernel, out_shape=(jax.ShapeDtypeStruct((SPECTRAL...]
where the time goes in v3:
time: 50.3 us; the launch traced here: 50.1 us
  Pallas kernels  42.6 us (85%)
  between operations  3 us (6%)
  starting transfers between devices  2.88 us (6%)
  local copies, waits for them, and re-layouts  1.69 us (3%)
    pallas_call x1, Pallas kernels, exchange(): pl.pallas_call(exchange_kernel, out_shape=(jax.ShapeDtypeStruct((SPECTRAL...  40.7 us
    ppermute x1, starting transfers between devices, local(): other = lax.ppermute(shared, 'chan', [(0, 1), (1, 0)])  2.88 us
    pallas_call x1, Pallas kernels, final(): pl.pallas_call(final_kernel, out_shape=jax.ShapeDtypeStruct((BAND_ROWS, 1...  1.81 us
    unnamed x4, local copies, waits for them, and re-layouts  1.69 us
  transfers between devices with their start and end apart: 1, of which 0 were waited for; matrix products, arithmetic and copies ran while one was open for 0% of the time, Pallas kernels for 4%

profile of v3, /device:TPU:1, one launch (start us, length us, event | category | flops | bytes accessed | tf_op | source)
XLA Modules:
  0.0 50.1 jit_solution(17897613940240033996)
XLA Ops:
  0.6 0.0 copy-start
  0.6 1.0 %copy-done = bf16[1,1,90,1440]{3,2,1,0:T(8,128)(2,1)S(1)} copy-done((bf16[1,1,90,1440]{3,2,1,0:T(8,128)(2,1)S(1)}, bf16[1,1,90,1440]{3,2,1,0:T(8,128)(2,1)}, u32[]{:S(2)}) %copy-start) | copy-done | bytes 259224
  1.6 0.0 copy-start.1
  1.6 0.7 %copy-done.1 = bf16[1,90,90]{2,1,0:T(8,128)(2,1)S(1)} copy-done((bf16[1,90,90]{2,1,0:T(8,128)(2,1)S(1)}, bf16[1,90,90]{2,1,0:T(8,128)(2,1)}, u32[]{:S(2)}) %copy-start.1) | copy-done | bytes 16224
  2.3 40.7 %shard_map.41 = (bf16[768,1536]{1,0:T(8,128)(2,1)S(1)}, bf16[128,3,2,128]{3,2,1,0:T(2,128)(2,1)S(1)}, bf16[16,9,8,128]{3,2,1,0:T(8,128)(2,1)S(1)}, f32[1,1]{1,0:T(1,128)}) custom-call(bf16[90,1440]{1,0:T(8,128)(2,1)S(1)} %bitcast.8, bf16[90,90]{1,0:T(8,128)(2,1)S(1)} %bitcast.9), custom_call_target="tpu_custom_call" | custom-call | flops 800000000 | bytes 8388608 | tf_op jit(solution)/shard_map/pallas_call | solution.py:472
  43.1 2.9 %collective-permute-start = (f32[1,1]{1,0:T(1,128)}, f32[1,1]{1,0:T(1,128)}, u32[]{:S(2)}, u32[]{:S(2)}) collective-permute-start(f32[1,1]{1,0:T(1,128)} %get-tuple-element.9), channel_id=1, source_target_pairs={{0,128},{128,0},{1,129},{129,1},{2,130},{130,2},{3,131},{131,3},{4... | collective-permute-start | bytes 20 | tf_op jit(solution)/shard_map/ppermute | solution.py:553
  46.0 1.8 %shard_map.42 = f32[90,1,1440]{2,1,0:T(1,128)} custom-call(bf16[768,1536]{1,0:T(8,128)(2,1)S(1)} %get-tuple-element.6.table_ref, bf16[768,128]{1,0:T(8,128)(2,1)S(1)} %bitcast.7, bf16[16,9,8,128]{3,2,1,0:T(8,128)(2,1)S(1)} %get-tuple-element.8.counts_ref), custom_call_target="tpu_custom_call" | custom-call | flops 400000000 | bytes 4194304 | tf_op jit(solution)/shard_map/pallas_call | solution.py:540
  47.8 0.0 collective-permute-done
Async XLA Ops:
  0.6 1.0 %copy-start = (bf16[1,1,90,1440]{3,2,1,0:T(8,128)(2,1)S(1)}, bf16[1,1,90,1440]{3,2,1,0:T(8,128)(2,1)}, u32[]{:S(2)}) copy-start(bf16[1,1,90,1440]{3,2,1,0:T(8,128)(2,1)} %param.2) | copy-start | bytes 777604
  1.6 0.7 %copy-start.1 = (bf16[1,90,90]{2,1,0:T(8,128)(2,1)S(1)}, bf16[1,90,90]{2,1,0:T(8,128)(2,1)}, u32[]{:S(2)}) copy-start(bf16[1,90,90]{2,1,0:T(8,128)(2,1)} %param.3) | copy-start | bytes 48604
  43.1 4.7 %collective-permute-start = (f32[1,1]{1,0:T(1,128)}, f32[1,1]{1,0:T(1,128)}, u32[]{:S(2)}, u32[]{:S(2)}) collective-permute-start(f32[1,1]{1,0:T(1,128)} %get-tuple-element.9), channel_id=1, source_target_pairs={{0,128},{128,0},{1,129},{129,1},{2,130},{130,2},{3,131},{131,3},{4... | collective-permute-start | bytes 20 | tf_op jit(solution)/shard_map/ppermute | solution.py:553

commit v4 on v3

--- a/solution.py
+++ b/solution.py
@@ -31,6 +31,7 @@
 PACKED_ROWS = GROUP_ROWS * LON_CHUNKS
 PACKED_TILES = PACKED_ROWS // 8
 PARTS = 2 * ORDERS
+FAR_FIRST = (2, 1, 3, 0)
 
 VMEM = pltpu.VMEM
 MESH = pl.DeviceIdType.MESH
@@ -215,7 +216,7 @@
     return lax.fori_loop(0, PACKED_TILES, body, jnp.zeros((8, LANES), F32))
 
 
-def spectral_stage(first, grid_loss, modes_ref, table_ref, out_ref, wide_ref, lhs_ref):
+def spectral_stage(first, grid_loss, modes_ref, table_ref, wide_ref, lhs_ref):
     draws = MEMBERS
     scale = SPECTRAL_WEIGHT * PARALLEL_LINES * AZIMUTH_STEPS / (DEGREE_CUTOFF * (DEGREE_CUTOFF + 1) / 2)
     held = BANDS * PARTS
@@ -287,10 +288,7 @@
     high, middle, low = (v.reshape(1, 1, 1, 1) for v in (high, middle, low))
     spare = jnp.where(column == LANES - 8, high, jnp.where(column == LANES - 7, middle, low))
     carries = (row == 0) & (column >= LANES - 8) & (column < LANES - 5)
-    for member in range(draws):
-        value = wide_ref[held * member : held * (member + 1), :].reshape(BANDS, ORDERS, 2, LANES)
-        value = jnp.where(carries, spare, value)
-        out_ref[BANDS * member : BANDS * (member + 1)] = value.astype(BF16)
+    return spare, carries
 
 
 def exchange_kernel(
@@ -328,6 +326,8 @@
     chan, ens, lat = lax.axis_index("chan"), lax.axis_index("ens"), lax.axis_index("lat")
     mine = ens * BANDS + lat
     first = ORDERS * mine
+    y, x = lax.div(ens, 4), lax.rem(lat, 4)
+    z = lax.div(lat, 4) * 4 + lax.rem(ens, 4)
     truth_copy = pltpu.make_async_copy(truth_hbm_ref, truth_in_ref, local_sem.at[0])
     truth_copy.start()
     own_copy = pltpu.make_async_copy(own_hbm_ref, own_ref, local_sem.at[1])
@@ -359,24 +359,39 @@
 
     def to_members(source, target, kind):
         def body(step, carry):
-            peer = lax.rem(ens + step, MEMBERS)
-            copy(source.at[peer], target.at[ens], kind, peer, lat).start()
+            peer_y = lax.rem(y + FAR_FIRST[0] + lax.div(step, 4), 4)
+            peer = peer_y * 4 + lax.rem(ens + 2 + step, 4)
+
+            @pl.when(peer != ens)
+            def _():
+                copy(source.at[peer], target.at[ens], kind, peer, lat).start()
+
             return carry
 
-        lax.fori_loop(1, MEMBERS, body, 0)
+        lax.fori_loop(0, MEMBERS, body, 0)
         target[ens] = source[ens]
 
-    def to_groups(source, target, kind, block):
+    def to_groups(source, target, kind, y_step):
+        peer_y = lax.rem(y + y_step, 4)
+
+        def send(z_step, x_step):
+            peer_z, peer_x = lax.rem(z + z_step, 8), lax.rem(x + x_step, 4)
+            peer_ens = peer_y * 4 + lax.rem(peer_z, 4)
+            peer_lat = lax.div(peer_z, 4) * 4 + peer_x
+            copy(
+                source.at[peer_ens * BANDS + peer_lat], target.at[mine], kind, peer_ens, peer_lat
+            ).start()
+
         def body(step, carry):
-            peer = block * 32 + lax.rem(mine + step, 32)
-
-            @pl.when(peer != mine)
-            def _():
-                copy(source.at[peer], target.at[mine], kind, lax.div(peer, BANDS), lax.rem(peer, BANDS)).start()
-
+            z_step = 4 + lax.div(step + 1, 2) * (1 - 2 * lax.rem(step, 2))
+            for x_step in FAR_FIRST:
+                send(z_step, x_step)
             return carry
 
-        lax.fori_loop(0, 32, body, 0)
+        lax.fori_loop(0, 8 if y_step else 7, body, 0)
+        if y_step == 0:
+            for x_step in FAR_FIRST[:3]:
+                send(0, x_step)
 
     def all_of(source, target, kind, count):
         return copy(source.at[pl.ds(0, count)], target.at[pl.ds(0, count)], kind, ens, lat)
@@ -388,8 +403,6 @@
     for group in range(ROW_GROUPS):
         blocks_out_ref[group] = wide_own_ref[GROUP_ROWS * group : GROUP_ROWS * group + 8, 0:LANES].astype(BF16)
     blocks_out_ref[ROW_GROUPS] = jnp.zeros((8, LANES), BF16)
-    pl.semaphore_wait(barrier, GROUPS - 1)
-    to_members(blocks_out_ref, blocks_in_ref, 0)
 
     own_copy.wait()
     wide_own_ref[0:BAND_ROWS, 0:AZIMUTH_STEPS] = own_ref[...].astype(F32)
@@ -400,7 +413,6 @@
             ]
         rows_out_ref[group] = packed_ref[...].reshape(PACKED_TILES, 8, LANES).astype(BF16)
     rows_out_ref[ROW_GROUPS] = jnp.zeros((PACKED_TILES, 8, LANES), BF16)
-    to_members(rows_out_ref, rows_in_ref, 1)
 
     fill_recurrence(first, coef_vector_ref)
     coef_copy = pltpu.make_async_copy(coef_vector_ref, coef_ref, local_sem.at[2])
@@ -412,13 +424,17 @@
         field_ref[16 * pair : 16 * pair + 16, :] = jnp.concatenate(both, axis=0).astype(BF16)
     fill_dft(dft_ref)
 
+    pl.semaphore_wait(barrier, GROUPS - 1)
+    to_members(blocks_out_ref, blocks_in_ref, 0)
+    to_members(rows_out_ref, rows_in_ref, 1)
+
     all_of(blocks_out_ref, blocks_in_ref, 0, MEMBERS - 1).wait_recv()
     fill_truth(blocks_in_ref, truth_ref, truth_packed_ref)
     both = [wide_own_ref[84:92, :], truth_ref[...]]
     field_ref[112:128, :] = jnp.concatenate(both, axis=0).astype(BF16)
 
-    def fourier(step, carry):
-        block = lax.rem(lax.div(mine, 32) + step, 4)
+    for y_step in FAR_FIRST:
+        block = lax.rem(y + y_step, 4)
         modes = lax.dot_general(
             dft_ref[pl.ds(pl.multiple_of(block * 192, 192), 192), :],
             field_ref[...],
@@ -426,10 +442,7 @@
             preferred_element_type=F32,
         )
         modes_out_ref[pl.ds(block * 32, 32)] = modes.reshape(32, ORDERS, 2, LANES).astype(BF16)
-        to_groups(modes_out_ref, modes_in_ref, 2, block)
-        return carry
-
-    lax.fori_loop(0, 4, fourier, 0)
+        to_groups(modes_out_ref, modes_in_ref, 2, y_step)
     modes_in_ref[mine] = modes_out_ref[mine]
 
     coef_copy.wait()
@@ -440,13 +453,16 @@
     to_members(counts_out_ref, counts_in_ref, 3)
 
     all_of(modes_out_ref, modes_in_ref, 2, GROUPS - 1).wait_recv()
-    spectral_stage(first, grid_loss, modes_in_ref, legendre_ref, back_out_ref, wide_ref, lhs_ref)
-
-    def give_back(step, carry):
-        to_groups(back_out_ref, back_in_ref, 4, lax.rem(lax.div(mine, 32) + step, 4))
-        return carry
-
-    lax.fori_loop(0, 4, give_back, 0)
+    spare, carries = spectral_stage(first, grid_loss, modes_in_ref, legendre_ref, wide_ref, lhs_ref)
+    held = BANDS * PARTS
+    for y_step in FAR_FIRST:
+        block = lax.rem(y + y_step, 4)
+        for part in range(4):
+            member = block * 4 + part
+            value = wide_ref[pl.ds(pl.multiple_of(member * held, held), held), :]
+            value = jnp.where(carries, spare, value.reshape(BANDS, ORDERS, 2, LANES))
+            back_out_ref[pl.ds(member * BANDS, BANDS)] = value.astype(BF16)
+        to_groups(back_out_ref, back_in_ref, 4, y_step)
     back_in_ref[mine] = back_out_ref[mine]
 
     all_of(counts_out_ref, counts_in_ref, 3, MEMBERS - 1).wait_recv()
@@ -549,7 +565,7 @@
 
 
 def local(model_outputs, verifying_truth):
-    table, back, counts, shared = exchange(model_outputs[0, 0], verifying_truth[0])
+    table, back, counts, shared = exchange(pltpu.with_memory_space_constraint(model_outputs[0, 0], pltpu.HBM), pltpu.with_memory_space_constraint(verifying_truth[0], pltpu.HBM))
     other = lax.ppermute(shared, "chan", [(0, 1), (1, 0)])
     slope = final(table, back.reshape(SPECTRAL_ROWS, LANES), counts)
     return (slope.reshape(1, 1, BAND_ROWS, AZIMUTH_STEPS), (shared + other)[0, 0])

time: 50.3 us -> 47.2 us (0.938)
  Pallas kernels: 42.6 us -> 40.7 us
  local copies, waits for them, and re-layouts: 1.69 us -> 0 us
    pallas_call x1, Pallas kernels: 40.7 us -> 38.9 us  [exchange(): pl.pallas_call(exchange_kernel, out_shape=(jax.ShapeDtypeStruct((SPECTRAL...]
    unnamed x4 -> x0, local copies, waits for them, and re-layouts: 1.69 us -> none
where the time goes in v4:
time: 47.2 us; the launch traced here: 47 us
  Pallas kernels  40.7 us (86%)
  starting transfers between devices  3.33 us (7%)
  between operations  3.03 us (6%)
    pallas_call x1, Pallas kernels, exchange(): pl.pallas_call(exchange_kernel, out_shape=(jax.ShapeDtypeStruct((SPECTRAL...  38.9 us
    ppermute x1, starting transfers between devices, local(): other = lax.ppermute(shared, 'chan', [(0, 1), (1, 0)])  3.33 us
    pallas_call x1, Pallas kernels, final(): pl.pallas_call(final_kernel, out_shape=jax.ShapeDtypeStruct((BAND_ROWS, 1...  1.74 us
  transfers between devices with their start and end apart: 1, of which 0 were waited for; matrix products, arithmetic and copies ran while one was open for 0% of the time, Pallas kernels for 4%

profile of v4, /device:TPU:1, one launch (start us, length us, event | category | flops | bytes accessed | tf_op | source)
XLA Modules:
  0.0 47.0 jit_solution(16983977740921568860)
XLA Ops:
  0.6 38.9 %shard_map.41 = (bf16[768,1536]{1,0:T(8,128)(2,1)S(1)}, bf16[128,3,2,128]{3,2,1,0:T(2,128)(2,1)S(1)}, bf16[16,9,8,128]{3,2,1,0:T(8,128)(2,1)S(1)}, f32[1,1]{1,0:T(1,128)}) custom-call(bf16[90,1440]{1,0:T(8,128)(2,1)} %bitcast.9, bf16[90,90]{1,0:T(8,128)(2,1)} %bitcast.10), custom_call_target="tpu_custom_call" | custom-call | flops 800000000 | bytes 8388608 | tf_op jit(solution)/shard_map/pallas_call | solution.py:488
  39.6 3.3 %collective-permute-start = (f32[1,1]{1,0:T(1,128)}, f32[1,1]{1,0:T(1,128)}, u32[]{:S(2)}, u32[]{:S(2)}) collective-permute-start(f32[1,1]{1,0:T(1,128)} %get-tuple-element.9), channel_id=1, source_target_pairs={{0,128},{128,0},{1,129},{129,1},{2,130},{130,2},{3,131},{131,3},{4... | collective-permute-start | bytes 20 | tf_op jit(solution)/shard_map/ppermute | solution.py:569
  42.9 1.7 %shard_map.42 = f32[90,1,1440]{2,1,0:T(1,128)} custom-call(bf16[768,1536]{1,0:T(8,128)(2,1)S(1)} %get-tuple-element.6.table_ref, bf16[768,128]{1,0:T(8,128)(2,1)S(1)} %bitcast.7, bf16[16,9,8,128]{3,2,1,0:T(8,128)(2,1)S(1)} %get-tuple-element.8.counts_ref), custom_call_target="tpu_custom_call" | custom-call | flops 400000000 | bytes 4194304 | tf_op jit(solution)/shard_map/pallas_call | solution.py:556
  44.6 0.0 collective-permute-done
Async XLA Ops:
  39.6 5.1 %collective-permute-start = (f32[1,1]{1,0:T(1,128)}, f32[1,1]{1,0:T(1,128)}, u32[]{:S(2)}, u32[]{:S(2)}) collective-permute-start(f32[1,1]{1,0:T(1,128)} %get-tuple-element.9), channel_id=1, source_target_pairs={{0,128},{128,0},{1,129},{129,1},{2,130},{130,2},{3,131},{131,3},{4... | collective-permute-start | bytes 20 | tf_op jit(solution)/shard_map/ppermute | solution.py:569

commit v5 on v4

--- a/solution.py
+++ b/solution.py
@@ -216,7 +216,7 @@
     return lax.fori_loop(0, PACKED_TILES, body, jnp.zeros((8, LANES), F32))
 
 
-def spectral_stage(first, grid_loss, modes_ref, table_ref, wide_ref, lhs_ref):
+def spectral_stage(first, grid_loss, modes_ref, table_ref, wide_ref, lhs_ref, result_ref):
     draws = MEMBERS
     scale = SPECTRAL_WEIGHT * PARALLEL_LINES * AZIMUTH_STEPS / (DEGREE_CUTOFF * (DEGREE_CUTOFF + 1) / 2)
     held = BANDS * PARTS
@@ -240,6 +240,7 @@
             aim = PARTS * band + 2 * index
             aims = [target[aim + r : aim + r + 1, :] for r in range(2)]
             lhs_ref[index, :, lanes] = jnp.concatenate(parts + aims + [pad], axis=0).astype(BF16)
+    for index in range(ORDERS):
         terms = lax.dot_general(
             lhs_ref[index],
             table_ref[index],
@@ -274,7 +275,7 @@
         back = jnp.dot(grad, table_ref[index], preferred_element_type=F32)
         for band in range(BANDS):
             for r in range(2):
-                wide_ref[pl.ds(PARTS * band + 2 * index + r, draws, stride=held), :] = back[
+                result_ref[pl.ds(PARTS * band + 2 * index + r, draws, stride=held), :] = back[
                     draws * r : draws * (r + 1), LANES * band : LANES * (band + 1)
                 ]
     local = jnp.sum(jnp.sum(grid_loss, axis=0, keepdims=True), axis=1, keepdims=True) / (
@@ -296,7 +297,7 @@
     truth_hbm_ref,
     dft_ref,
     back_in_ref,
-    counts_in_ref,
+    base_ref,
     loss_ref,
     own_ref,
     truth_in_ref,
@@ -316,9 +317,11 @@
     table_ref,
     legendre_ref,
     counts_out_ref,
+    counts_in_ref,
     back_out_ref,
     wide_ref,
     lhs_ref,
+    result_ref,
     send_sem,
     recv_sem,
     local_sem,
@@ -335,17 +338,31 @@
 
     barrier = pltpu.get_barrier_semaphore()
 
-    def greet(step, carry):
-        peer = lax.rem(mine + step, GROUPS)
+    def each_group(y_step, visit):
+        peer_y = lax.rem(y + y_step, 4)
+
+        def one(z_step, x_step):
+            peer_z, peer_x = lax.rem(z + z_step, 8), lax.rem(x + x_step, 4)
+            visit(peer_y * 4 + lax.rem(peer_z, 4), lax.div(peer_z, 4) * 4 + peer_x)
+
+        def body(step, carry):
+            z_step = 4 + lax.div(step + 1, 2) * (1 - 2 * lax.rem(step, 2))
+            for x_step in FAR_FIRST:
+                one(z_step, x_step)
+            return carry
+
+        lax.fori_loop(0, 8 if y_step else 7, body, 0)
+        if y_step == 0:
+            for x_step in FAR_FIRST[:3]:
+                one(0, x_step)
+
+    def greet(peer_ens, peer_lat):
         pl.semaphore_signal(
-            barrier,
-            inc=1,
-            device_id=(chan, lax.div(peer, BANDS), lax.rem(peer, BANDS)),
-            device_id_type=MESH,
-        )
-        return carry
-
-    lax.fori_loop(1, GROUPS, greet, 0)
+            barrier, inc=1, device_id=(chan, peer_ens, peer_lat), device_id_type=MESH
+        )
+
+    for y_step in FAR_FIRST:
+        each_group(y_step, greet)
 
     def copy(source, target, kind, peer_ens, peer_lat):
         return pltpu.make_async_remote_copy(
@@ -372,26 +389,12 @@
         target[ens] = source[ens]
 
     def to_groups(source, target, kind, y_step):
-        peer_y = lax.rem(y + y_step, 4)
-
-        def send(z_step, x_step):
-            peer_z, peer_x = lax.rem(z + z_step, 8), lax.rem(x + x_step, 4)
-            peer_ens = peer_y * 4 + lax.rem(peer_z, 4)
-            peer_lat = lax.div(peer_z, 4) * 4 + peer_x
+        def send(peer_ens, peer_lat):
             copy(
                 source.at[peer_ens * BANDS + peer_lat], target.at[mine], kind, peer_ens, peer_lat
             ).start()
 
-        def body(step, carry):
-            z_step = 4 + lax.div(step + 1, 2) * (1 - 2 * lax.rem(step, 2))
-            for x_step in FAR_FIRST:
-                send(z_step, x_step)
-            return carry
-
-        lax.fori_loop(0, 8 if y_step else 7, body, 0)
-        if y_step == 0:
-            for x_step in FAR_FIRST[:3]:
-                send(0, x_step)
+        each_group(y_step, send)
 
     def all_of(source, target, kind, count):
         return copy(source.at[pl.ds(0, count)], target.at[pl.ds(0, count)], kind, ens, lat)
@@ -453,19 +456,29 @@
     to_members(counts_out_ref, counts_in_ref, 3)
 
     all_of(modes_out_ref, modes_in_ref, 2, GROUPS - 1).wait_recv()
-    spare, carries = spectral_stage(first, grid_loss, modes_in_ref, legendre_ref, wide_ref, lhs_ref)
+    spare, carries = spectral_stage(
+        first, grid_loss, modes_in_ref, legendre_ref, wide_ref, lhs_ref, result_ref
+    )
     held = BANDS * PARTS
     for y_step in FAR_FIRST:
         block = lax.rem(y + y_step, 4)
         for part in range(4):
             member = block * 4 + part
-            value = wide_ref[pl.ds(pl.multiple_of(member * held, held), held), :]
+            value = result_ref[pl.ds(pl.multiple_of(member * held, held), held), :]
             value = jnp.where(carries, spare, value.reshape(BANDS, ORDERS, 2, LANES))
             back_out_ref[pl.ds(member * BANDS, BANDS)] = value.astype(BF16)
         to_groups(back_out_ref, back_in_ref, 4, y_step)
     back_in_ref[mine] = back_out_ref[mine]
 
     all_of(counts_out_ref, counts_in_ref, 3, MEMBERS - 1).wait_recv()
+    for group in range(ROW_GROUPS):
+        packed_ref[...] = counts_in_ref[group].astype(F32).reshape(PACKED_ROWS, LANES)
+        line = BAND_ROWS * lat + GROUP_ROWS * group + iota((8, LANES), 0)
+        weight = (cos_sin(line.astype(F32) + 0.5)[1] / (MEMBERS - 1))[0:GROUP_ROWS]
+        for chunk in range(LON_CHUNKS):
+            base_ref[8 * group : 8 * group + GROUP_ROWS, LANES * chunk : LANES * (chunk + 1)] = (
+                weight * packed_ref[GROUP_ROWS * chunk : GROUP_ROWS * (chunk + 1), :]
+            )
     all_of(back_out_ref, back_in_ref, 4, GROUPS - 1).wait_recv()
     total = jnp.zeros((2, LANES), F32)
     for block in range(16):
@@ -490,7 +503,7 @@
         out_shape=(
             jax.ShapeDtypeStruct((SPECTRAL_ROWS, LON_PADDED), BF16),
             jax.ShapeDtypeStruct(modes, BF16),
-            jax.ShapeDtypeStruct(rows, BF16),
+            jax.ShapeDtypeStruct((LANES, LON_PADDED), F32),
             jax.ShapeDtypeStruct((1, 1), F32),
         ),
         in_specs=[pl.BlockSpec(memory_space=pltpu.HBM)] * 2,
@@ -514,9 +527,11 @@
             VMEM((ORDERS * DEGREE_CUTOFF * 8, LANES), F32),
             VMEM((ORDERS, DEGREE_CUTOFF, BANDS * LANES), BF16),
             VMEM(rows, BF16),
+            VMEM(rows, BF16),
             VMEM(modes, BF16),
             VMEM((SPECTRAL_ROWS, LANES), F32),
             VMEM((ORDERS, 48, BANDS * LANES), BF16),
+            VMEM((SPECTRAL_ROWS, LANES), F32),
             pltpu.SemaphoreType.DMA((5,)),
             pltpu.SemaphoreType.DMA((5,)),
             pltpu.SemaphoreType.DMA((3,)),
@@ -526,14 +541,7 @@
     )(own, target)
 
 
-def final_kernel(table_ref, modes_ref, counts_ref, out_ref, packed_ref):
-    row = iota((LANES, LANES), 0)
-    line = BAND_ROWS * lax.axis_index("lat") + GROUP_ROWS * (row >> 3) + (row & 7)
-    weight = cos_sin(line.astype(F32) + 0.5)[1] / (MEMBERS - 1)
-    for group in range(ROW_GROUPS):
-        packed_ref[PACKED_ROWS * group : PACKED_ROWS * (group + 1), :] = (
-            counts_ref[group].astype(F32).reshape(PACKED_ROWS, LANES)
-        )
+def final_kernel(table_ref, modes_ref, base_ref, out_ref):
     for chunk in range(LON_CHUNKS):
         lanes = slice(LANES * chunk, LANES * (chunk + 1))
         width = min(LANES, AZIMUTH_STEPS - LANES * chunk)
@@ -544,30 +552,28 @@
             preferred_element_type=F32,
         )
         for group in range(ROW_GROUPS):
-            first = PACKED_ROWS * group + GROUP_ROWS * chunk
             rows = slice(8 * group, 8 * group + GROUP_ROWS)
-            total = weight[rows] * packed_ref[first : first + GROUP_ROWS, :] + wave[rows]
+            total = base_ref[rows, lanes] + wave[rows]
             out_ref[
                 GROUP_ROWS * group : GROUP_ROWS * (group + 1), 0, LANES * chunk : LANES * chunk + width
             ] = total[:, 0:width]
 
 
-def final(table, modes, counts):
+def final(table, modes, base):
     return pl.pallas_call(
         final_kernel,
         out_shape=jax.ShapeDtypeStruct((BAND_ROWS, 1, AZIMUTH_STEPS), F32),
         in_specs=[pl.BlockSpec(memory_space=VMEM)] * 3,
         out_specs=pl.BlockSpec(memory_space=VMEM),
-        scratch_shapes=[VMEM((ROW_GROUPS * PACKED_ROWS, LANES), F32)],
         compiler_params=params(),
         cost_estimate=pl.CostEstimate(flops=400_000_000, bytes_accessed=4 << 20, transcendentals=0),
-    )(table, modes, counts)
+    )(table, modes, base)
 
 
 def local(model_outputs, verifying_truth):
-    table, back, counts, shared = exchange(pltpu.with_memory_space_constraint(model_outputs[0, 0], pltpu.HBM), pltpu.with_memory_space_constraint(verifying_truth[0], pltpu.HBM))
+    table, back, base, shared = exchange(pltpu.with_memory_space_constraint(model_outputs[0, 0], pltpu.HBM), pltpu.with_memory_space_constraint(verifying_truth[0], pltpu.HBM))
     other = lax.ppermute(shared, "chan", [(0, 1), (1, 0)])
-    slope = final(table, back.reshape(SPECTRAL_ROWS, LANES), counts)
+    slope = final(table, back.reshape(SPECTRAL_ROWS, LANES), base)
     return (slope.reshape(1, 1, BAND_ROWS, AZIMUTH_STEPS), (shared + other)[0, 0])
 
 

time: 47.2 us -> 46.2 us (0.979)
  Pallas kernels: 40.7 us -> 39.8 us
    pallas_call x1, Pallas kernels: 38.9 us -> 38.1 us  [exchange(): pl.pallas_call(exchange_kernel, out_shape=(jax.ShapeDtypeStruct((SPECTRAL...]
where the time goes in v5:
time: 46.2 us; the launch traced here: 46.1 us
  Pallas kernels  39.8 us (86%)
  starting transfers between devices  3.28 us (7%)
  between operations  3.03 us (7%)
    pallas_call x1, Pallas kernels, exchange(): pl.pallas_call(exchange_kernel, out_shape=(jax.ShapeDtypeStruct((SPECTRAL...  38.1 us
    ppermute x1, starting transfers between devices, local(): other = lax.ppermute(shared, 'chan', [(0, 1), (1, 0)])  3.28 us
    pallas_call x1, Pallas kernels, final(): pl.pallas_call(final_kernel, out_shape=jax.ShapeDtypeStruct((BAND_ROWS, 1...  1.67 us
  transfers between devices with their start and end apart: 1, of which 0 were waited for; matrix products, arithmetic and copies ran while one was open for 0% of the time, Pallas kernels for 4%

profile of v5, /device:TPU:1, one launch (start us, length us, event | category | flops | bytes accessed | tf_op | source)
XLA Modules:
  0.0 46.1 jit_solution(17747543220266951008)
XLA Ops:
  0.6 38.1 %shard_map.41 = (bf16[768,1536]{1,0:T(8,128)(2,1)S(1)}, bf16[128,3,2,128]{3,2,1,0:T(2,128)(2,1)S(1)}, f32[128,1536]{1,0:T(8,128)S(1)}, f32[1,1]{1,0:T(1,128)}) custom-call(bf16[90,1440]{1,0:T(8,128)(2,1)} %bitcast.9, bf16[90,90]{1,0:T(8,128)(2,1)} %bitcast.10), custom_call_target="tpu_custom_call" | custom-call | flops 800000000 | bytes 8388608 | tf_op jit(solution)/shard_map/pallas_call | solution.py:501
  38.7 3.3 %collective-permute-start = (f32[1,1]{1,0:T(1,128)}, f32[1,1]{1,0:T(1,128)}, u32[]{:S(2)}, u32[]{:S(2)}) collective-permute-start(f32[1,1]{1,0:T(1,128)} %get-tuple-element.9), channel_id=1, source_target_pairs={{0,128},{128,0},{1,129},{129,1},{2,130},{130,2},{3,131},{131,3},{4... | collective-permute-start | bytes 20 | tf_op jit(solution)/shard_map/ppermute | solution.py:575
  42.0 1.7 %shard_map.42 = f32[90,1,1440]{2,1,0:T(1,128)} custom-call(bf16[768,1536]{1,0:T(8,128)(2,1)S(1)} %get-tuple-element.6.table_ref, bf16[768,128]{1,0:T(8,128)(2,1)S(1)} %bitcast.7, f32[128,1536]{1,0:T(8,128)S(1)} %get-tuple-element.8.base_ref), custom_call_target="tpu_custom_call" | custom-call | flops 400000000 | bytes 4194304 | tf_op jit(solution)/shard_map/pallas_call | solution.py:563
  43.7 0.0 collective-permute-done
Async XLA Ops:
  38.7 4.9 %collective-permute-start = (f32[1,1]{1,0:T(1,128)}, f32[1,1]{1,0:T(1,128)}, u32[]{:S(2)}, u32[]{:S(2)}) collective-permute-start(f32[1,1]{1,0:T(1,128)} %get-tuple-element.9), channel_id=1, source_target_pairs={{0,128},{128,0},{1,129},{129,1},{2,130},{130,2},{3,131},{131,3},{4... | collective-permute-start | bytes 20 | tf_op jit(solution)/shard_map/ppermute | solution.py:575

commit v6 on v5

--- a/solution.py
+++ b/solution.py
@@ -118,7 +118,7 @@
     return 0.5 * jnp.log(order[:, 0:1] + 0.5) + 0.5 * jnp.sum(summands, axis=1, keepdims=True)
 
 
-def fill_legendre(first, coef_ref, table_ref, out_ref):
+def legendre_recurrence(first, coef_ref, table_ref):
     band, lane = iota((8, LANES), 0), iota((8, LANES), 1)
     group, part = lane >> 3, lane & 7
     valid = (group < ROW_GROUPS) & (part < GROUP_ROWS)
@@ -161,6 +161,9 @@
         start = jnp.broadcast_to(seeds[index : index + 1, :], (8, LANES)) + order * log_sin
         state += [jnp.zeros((8, LANES), F32), jnp.zeros((8, LANES), F32), start, jnp.exp(start) * weight]
     lax.fori_loop(0, DEGREE_CUTOFF // BLOCK, body, tuple(state))
+
+
+def fill_legendre(table_ref, out_ref):
     for index in range(ORDERS):
         for band in range(BANDS):
             rows = table_ref[pl.ds(index * DEGREE_CUTOFF * 8 + band, DEGREE_CUTOFF, stride=8), :]
@@ -417,6 +420,9 @@
         rows_out_ref[group] = packed_ref[...].reshape(PACKED_TILES, 8, LANES).astype(BF16)
     rows_out_ref[ROW_GROUPS] = jnp.zeros((PACKED_TILES, 8, LANES), BF16)
 
+    pl.semaphore_wait(barrier, GROUPS - 1)
+    to_members(blocks_out_ref, blocks_in_ref, 0)
+    to_members(rows_out_ref, rows_in_ref, 1)
     fill_recurrence(first, coef_vector_ref)
     coef_copy = pltpu.make_async_copy(coef_vector_ref, coef_ref, local_sem.at[2])
     coef_copy.start()
@@ -426,10 +432,6 @@
         ]
         field_ref[16 * pair : 16 * pair + 16, :] = jnp.concatenate(both, axis=0).astype(BF16)
     fill_dft(dft_ref)
-
-    pl.semaphore_wait(barrier, GROUPS - 1)
-    to_members(blocks_out_ref, blocks_in_ref, 0)
-    to_members(rows_out_ref, rows_in_ref, 1)
 
     all_of(blocks_out_ref, blocks_in_ref, 0, MEMBERS - 1).wait_recv()
     fill_truth(blocks_in_ref, truth_ref, truth_packed_ref)
@@ -449,7 +451,8 @@
     modes_in_ref[mine] = modes_out_ref[mine]
 
     coef_copy.wait()
-    fill_legendre(first, coef_ref, table_ref, legendre_ref)
+    legendre_recurrence(first, coef_ref, table_ref)
+    fill_legendre(table_ref, legendre_ref)
 
     all_of(rows_out_ref, rows_in_ref, 1, MEMBERS - 1).wait_recv()
     grid_loss = grid_stage(ens, lat, rows_in_ref, truth_packed_ref, counts_out_ref)
@@ -542,21 +545,18 @@
 
 
 def final_kernel(table_ref, modes_ref, base_ref, out_ref):
-    for chunk in range(LON_CHUNKS):
-        lanes = slice(LANES * chunk, LANES * (chunk + 1))
-        width = min(LANES, AZIMUTH_STEPS - LANES * chunk)
-        wave = lax.dot_general(
-            modes_ref[...],
-            table_ref[:, lanes],
-            (((0,), (0,)), ((), ())),
-            preferred_element_type=F32,
-        )
+    modes = modes_ref[...].astype(F32).T.astype(BF16)
+    for chunk in range(LON_CHUNKS // 2):
+        first = 2 * LANES * chunk
+        lanes = slice(first, first + 2 * LANES)
+        width = min(2 * LANES, AZIMUTH_STEPS - first)
+        wave = jnp.dot(modes, table_ref[:, lanes], preferred_element_type=F32)
         for group in range(ROW_GROUPS):
             rows = slice(8 * group, 8 * group + GROUP_ROWS)
             total = base_ref[rows, lanes] + wave[rows]
-            out_ref[
-                GROUP_ROWS * group : GROUP_ROWS * (group + 1), 0, LANES * chunk : LANES * chunk + width
-            ] = total[:, 0:width]
+            out_ref[GROUP_ROWS * group : GROUP_ROWS * (group + 1), 0, first : first + width] = total[
+                :, 0:width
+            ]
 
 
 def final(table, modes, base):

time: 46.2 us -> 45.9 us (level)
  transfers between devices with their start and end apart: 1 -> 1, of which waited for: 0 -> 0; matrix products, arithmetic and copies ran while one was open for 0% -> 0% of each run, Pallas kernels for 4% -> 3%
where the time goes in v6:
time: 45.9 us; the launch traced here: 45.8 us
  Pallas kernels  39.5 us (86%)
  starting transfers between devices  3.31 us (7%)
  between operations  3.03 us (7%)
    pallas_call x1, Pallas kernels, exchange(): pl.pallas_call(exchange_kernel, out_shape=(jax.ShapeDtypeStruct((SPECTRAL...  38.1 us
    ppermute x1, starting transfers between devices, local(): other = lax.ppermute(shared, 'chan', [(0, 1), (1, 0)])  3.31 us
    pallas_call x1, Pallas kernels, final(): pl.pallas_call(final_kernel, out_shape=jax.ShapeDtypeStruct((BAND_ROWS, 1...  1.39 us
  transfers between devices with their start and end apart: 1, of which 0 were waited for; matrix products, arithmetic and copies ran while one was open for 0% of the time, Pallas kernels for 3%

profile of v6, /device:TPU:1, one launch (start us, length us, event | category | flops | bytes accessed | tf_op | source)
XLA Modules:
  0.0 45.8 jit_solution(12453853977070567684)
XLA Ops:
  0.6 38.1 %shard_map.41 = (bf16[768,1536]{1,0:T(8,128)(2,1)S(1)}, bf16[128,3,2,128]{3,2,1,0:T(2,128)(2,1)S(1)}, f32[128,1536]{1,0:T(8,128)S(1)}, f32[1,1]{1,0:T(1,128)}) custom-call(bf16[90,1440]{1,0:T(8,128)(2,1)} %bitcast.9, bf16[90,90]{1,0:T(8,128)(2,1)} %bitcast.10), custom_call_target="tpu_custom_call" | custom-call | flops 800000000 | bytes 8388608 | tf_op jit(solution)/shard_map/pallas_call | solution.py:504
  38.7 3.3 %collective-permute-start = (f32[1,1]{1,0:T(1,128)}, f32[1,1]{1,0:T(1,128)}, u32[]{:S(2)}, u32[]{:S(2)}) collective-permute-start(f32[1,1]{1,0:T(1,128)} %get-tuple-element.9), channel_id=1, source_target_pairs={{0,128},{128,0},{1,129},{129,1},{2,130},{130,2},{3,131},{131,3},{4... | collective-permute-start | bytes 20 | tf_op jit(solution)/shard_map/ppermute | solution.py:575
  42.0 1.4 %shard_map.42 = f32[90,1,1440]{2,1,0:T(1,128)} custom-call(bf16[768,1536]{1,0:T(8,128)(2,1)S(1)} %get-tuple-element.6.table_ref, bf16[768,128]{1,0:T(8,128)(2,1)S(1)} %bitcast.7, f32[128,1536]{1,0:T(8,128)S(1)} %get-tuple-element.8.base_ref), custom_call_target="tpu_custom_call" | custom-call | flops 400000000 | bytes 4194304 | tf_op jit(solution)/shard_map/pallas_call | solution.py:563
  43.4 0.0 collective-permute-done
Async XLA Ops:
  38.7 4.7 %collective-permute-start = (f32[1,1]{1,0:T(1,128)}, f32[1,1]{1,0:T(1,128)}, u32[]{:S(2)}, u32[]{:S(2)}) collective-permute-start(f32[1,1]{1,0:T(1,128)} %get-tuple-element.9), channel_id=1, source_target_pairs={{0,128},{128,0},{1,129},{129,1},{2,130},{130,2},{3,131},{131,3},{4... | collective-permute-start | bytes 20 | tf_op jit(solution)/shard_map/ppermute | solution.py:575

commit v7 on v6

--- a/solution.py
+++ b/solution.py
@@ -410,6 +410,8 @@
         blocks_out_ref[group] = wide_own_ref[GROUP_ROWS * group : GROUP_ROWS * group + 8, 0:LANES].astype(BF16)
     blocks_out_ref[ROW_GROUPS] = jnp.zeros((8, LANES), BF16)
 
+    pl.semaphore_wait(barrier, GROUPS - 1)
+    to_members(blocks_out_ref, blocks_in_ref, 0)
     own_copy.wait()
     wide_own_ref[0:BAND_ROWS, 0:AZIMUTH_STEPS] = own_ref[...].astype(F32)
     for group in range(ROW_GROUPS):
@@ -419,9 +421,6 @@
             ]
         rows_out_ref[group] = packed_ref[...].reshape(PACKED_TILES, 8, LANES).astype(BF16)
     rows_out_ref[ROW_GROUPS] = jnp.zeros((PACKED_TILES, 8, LANES), BF16)
-
-    pl.semaphore_wait(barrier, GROUPS - 1)
-    to_members(blocks_out_ref, blocks_in_ref, 0)
     to_members(rows_out_ref, rows_in_ref, 1)
     fill_recurrence(first, coef_vector_ref)
     coef_copy = pltpu.make_async_copy(coef_vector_ref, coef_ref, local_sem.at[2])

time: 45.9 us -> 45.9 us (level)
  no operation moved by 1% of the time
where the time goes in v7:
time: 45.9 us; the launch traced here: 45.8 us
  Pallas kernels  39.9 us (87%)
  between operations  3.03 us (7%)
  starting transfers between devices  2.9 us (6%)
    pallas_call x1, Pallas kernels, exchange(): pl.pallas_call(exchange_kernel, out_shape=(jax.ShapeDtypeStruct((SPECTRAL...  38.5 us
    ppermute x1, starting transfers between devices, local(): other = lax.ppermute(shared, 'chan', [(0, 1), (1, 0)])  2.9 us
    pallas_call x1, Pallas kernels, final(): pl.pallas_call(final_kernel, out_shape=jax.ShapeDtypeStruct((BAND_ROWS, 1...  1.39 us
  transfers between devices with their start and end apart: 1, of which 0 were waited for; matrix products, arithmetic and copies ran while one was open for 0% of the time, Pallas kernels for 3%

profile of v7, /device:TPU:1, one launch (start us, length us, event | category | flops | bytes accessed | tf_op | source)
XLA Modules:
  0.0 45.8 jit_solution(944274543199661490)
XLA Ops:
  0.6 38.5 %shard_map.41 = (bf16[768,1536]{1,0:T(8,128)(2,1)S(1)}, bf16[128,3,2,128]{3,2,1,0:T(2,128)(2,1)S(1)}, f32[128,1536]{1,0:T(8,128)S(1)}, f32[1,1]{1,0:T(1,128)}) custom-call(bf16[90,1440]{1,0:T(8,128)(2,1)} %bitcast.9, bf16[90,90]{1,0:T(8,128)(2,1)} %bitcast.10), custom_call_target="tpu_custom_call" | custom-call | flops 800000000 | bytes 8388608 | tf_op jit(solution)/shard_map/pallas_call | solution.py:503
  39.1 2.9 %collective-permute-start = (f32[1,1]{1,0:T(1,128)}, f32[1,1]{1,0:T(1,128)}, u32[]{:S(2)}, u32[]{:S(2)}) collective-permute-start(f32[1,1]{1,0:T(1,128)} %get-tuple-element.9), channel_id=1, source_target_pairs={{0,128},{128,0},{1,129},{129,1},{2,130},{130,2},{3,131},{131,3},{4... | collective-permute-start | bytes 20 | tf_op jit(solution)/shard_map/ppermute | solution.py:574
  42.0 1.4 %shard_map.42 = f32[90,1,1440]{2,1,0:T(1,128)} custom-call(bf16[768,1536]{1,0:T(8,128)(2,1)S(1)} %get-tuple-element.6.table_ref, bf16[768,128]{1,0:T(8,128)(2,1)S(1)} %bitcast.7, f32[128,1536]{1,0:T(8,128)S(1)} %get-tuple-element.8.base_ref), custom_call_target="tpu_custom_call" | custom-call | flops 400000000 | bytes 4194304 | tf_op jit(solution)/shard_map/pallas_call | solution.py:562
  43.4 0.0 collective-permute-done
Async XLA Ops:
  39.1 4.3 %collective-permute-start = (f32[1,1]{1,0:T(1,128)}, f32[1,1]{1,0:T(1,128)}, u32[]{:S(2)}, u32[]{:S(2)}) collective-permute-start(f32[1,1]{1,0:T(1,128)} %get-tuple-element.9), channel_id=1, source_target_pairs={{0,128},{128,0},{1,129},{129,1},{2,130},{130,2},{3,131},{131,3},{4... | collective-permute-start | bytes 20 | tf_op jit(solution)/shard_map/ppermute | solution.py:574
